TPU v7x, 32 devices: a whole 2x2x4 slice. The times are simulated.
32 devices in a mesh: grp: 4 (over y, core), rep: 8 (over z, x).
Axes of the slice: x: 2, y: 2, z: 4, core: 2. Of those that a mesh axis runs over, the one named last changes fastest.
Arguments:
- tokens: bfloat16 [32, 1024, 768], P(('grp', 'rep')), may hold values from -6 to 6
- segment_ids: int32 [32, 1024], P(('grp', 'rep')), may hold values from 0 to 2, as said below
- cotangent: bfloat16 [32, 1024, 768], P(('grp', 'rep')), may hold values from -6 to 6
- in_proj_master: float32 [768, 3352], P('grp'), may hold values from -0.21875 to 0.21875
- out_proj_master: float32 [1536, 768], P('grp'), may hold values from -0.15625 to 0.15625
- in_proj_error: float32 [8, 768, 3352], P('rep', 'grp'), may hold values from -6 to 6
- out_proj_error: float32 [8, 1536, 768], P('rep', 'grp'), may hold values from -6 to 6
- in_proj_moment: float32 [768, 3352], P('grp'), may hold values from -6 to 6
- out_proj_moment: float32 [1536, 768], P('grp'), may hold values from -6 to 6
- in_proj_start: float32 [4, 3352, 8], P('grp'), may hold values from -6 to 6
- out_proj_start: float32 [4, 768, 8], P('grp'), may hold values from -6 to 6
- conv_master: float32 [5, 1792], replicated, may hold values from -3 to 3
- conv_moment: float32 [5, 1792], replicated, may hold values from -6 to 6
- head_master: float32 [3, 24], replicated, may hold values from -8 to 2, as said below
- head_moment: float32 [3, 24], replicated, may hold values from -6 to 6
- norm_gain: float32 [768], replicated, may hold values from 0.5 to 1.5
- norm_gain_moment: float32 [768], replicated, may hold values from -6 to 6
- gate_gain: float32 [1536], replicated, may hold values from 0.5 to 1.5
- gate_gain_moment: float32 [1536], replicated, may hold values from -6 to 6
Outputs:
- output: bfloat16 [32, 1024, 768], P(('grp', 'rep'))
- input_grad: float32 [32, 1024, 768], P(('grp', 'rep'))
- in_proj_grad: float32 [8, 768, 3352], P('rep', 'grp')
- out_proj_grad: float32 [8, 1536, 768], P('rep', 'grp')
- in_proj_left: float32 [768, 8], P('grp')
- out_proj_left: float32 [1536, 8], P('grp')
- in_proj_right: float32 [4, 3352, 8], P('grp')
- out_proj_right: float32 [4, 768, 8], P('grp')
- in_proj_error_new: float32 [8, 768, 3352], P('rep', 'grp')
- out_proj_error_new: float32 [8, 1536, 768], P('rep', 'grp')
- in_proj_moment_new: float32 [768, 3352], P('grp')
- out_proj_moment_new: float32 [1536, 768], P('grp')
- in_proj_master_new: float32 [768, 3352], P('grp')
- out_proj_master_new: float32 [1536, 768], P('grp')
- conv_grad: float32 [5, 1792], replicated
- conv_moment_new: float32 [5, 1792], replicated
- conv_master_new: float32 [5, 1792], replicated
- head_grad: float32 [3, 24], replicated
- head_moment_new: float32 [3, 24], replicated
- head_master_new: float32 [3, 24], replicated
- norm_gain_grad: float32 [768], replicated
- norm_gain_moment_new: float32 [768], replicated
- norm_gain_new: float32 [768], replicated
- gate_gain_grad: float32 [1536], replicated
- gate_gain_moment_new: float32 [1536], replicated
- gate_gain_new: float32 [1536], replicated
Inputs may be any that keep to these rules, and one draw needn't show every extreme that they name: `segment_ids`: within each sequence the ids never fall and all 3 ids occur; each document has 204 to 512 tokens and one has exactly 512. `head_master`: row 0 is the step bias, row 1 the log of the decay rate, row 2 the skip gain.
All inputs are finite; a program needn't handle non-finite values.
Results may differ from a plain program's by a relative error of at most 0.011.
Values may be sent and summed in bfloat16 or wider, within the bound.
No kernel may reach another device: no remote copies, remote signals or barrier semaphores. Data moves between devices by JAX's collectives and lax.ppermute only.
A program may use at most 256 MiB of HBM per device.

v0:
```python
import jax
import jax.numpy as jnp
from jax import lax
from jax.sharding import PartitionSpec as P

HEADS = 24
HEADDIM = 64
STATE = 128
CONV = 4
SPAN = 256
INNER = 1536
CONVDIM = 1792


EPS = 1e-05
GS_EPS = 1e-06
MOMENTUM = 0.9
RATE = 0.01
HIGH = lax.Precision.HIGHEST


def prenorm(inputs, gain):
    return inputs * lax.rsqrt(jnp.mean(inputs * inputs, axis=-1, keepdims=True) + EPS) * gain


def conv_part(projected, conv_params, head_params, segments):
    gate_in = projected[:, :INNER]
    conv_in = projected[:, INNER : INNER + CONVDIM]
    raw_steps = projected[:, INNER + CONVDIM :]
    summed = jnp.broadcast_to(conv_params[CONV], conv_in.shape)
    for offset in range(CONV):
        tap_row = conv_params[CONV - 1 - offset]
        if offset == 0:
            summed = summed + tap_row * conv_in
        else:
            shifted = jnp.pad(conv_in[:-offset], ((offset, 0), (0, 0)))
            earlier = jnp.pad(segments[:-offset], (offset, 0), constant_values=-1)
            same_doc = (earlier == segments).astype(jnp.float32)
            summed = summed + tap_row * shifted * same_doc[:, None]
    active = jax.nn.silu(summed)
    step_sizes = jax.nn.softplus(raw_steps + head_params[0])
    return (gate_in, active, step_sizes)


def span_step(carry, block):
    state, last_doc = carry
    values, sizes, decay_log, in_b, out_c, docs = block
    positions = docs.shape[0]
    heads_vals = values.reshape(positions, HEADS, HEADDIM)
    cumul = jnp.cumsum(decay_log, axis=1)
    places = jnp.arange(positions)
    allowed = (places[:, None] >= places[None, :]) & (docs[:, None] == docs[None, :])
    spread = cumul[:, :, None] - cumul[:, None, :]
    mask_three = allowed[None, :, :]
    decays = jnp.where(mask_three, jnp.exp(jnp.where(mask_three, spread, 0.0)), 0.0)
    inner_prod = jnp.dot(out_c, in_b.T, precision=HIGH)
    mixing = inner_prod[None, :, :] * decays * sizes[:, None, :]
    local_out = jnp.einsum("hij,jhp->ihp", mixing, heads_vals, precision=HIGH)
    alive = (docs == last_doc).astype(jnp.float32)
    carried = jnp.einsum("in,hpn->ihp", out_c, state, precision=HIGH)
    carried = carried * (jnp.exp(cumul).T * alive[:, None])[:, :, None]
    tail_weight = (
        jnp.exp(cumul[:, -1:] - cumul) * (docs == docs[-1]).astype(jnp.float32)[None, :] * sizes
    )
    keep_rate = jnp.exp(cumul[:, -1]) * (docs[-1] == last_doc).astype(jnp.float32)
    added = jnp.einsum("jhp,jn->hpn", tail_weight.T[:, :, None] * heads_vals, in_b, precision=HIGH)
    new_state = state * keep_rate[:, None, None] + added
    return ((new_state, docs[-1]), (local_out + carried).reshape(positions, INNER))


def spanned_scan(values, sizes, decay_log, in_b, out_c, segments):
    length = values.shape[0]
    blocks = length // SPAN
    pieces = (
        values.reshape(blocks, SPAN, INNER),
        jnp.swapaxes(sizes.reshape(blocks, SPAN, HEADS), 1, 2),
        jnp.swapaxes(decay_log.reshape(blocks, SPAN, HEADS), 1, 2),
        in_b.reshape(blocks, SPAN, STATE),
        out_c.reshape(blocks, SPAN, STATE),
        segments.reshape(blocks, SPAN),
    )
    start = (jnp.zeros((HEADS, HEADDIM, STATE), jnp.float32), jnp.array(-1, jnp.int32))
    ended, outputs = lax.scan(jax.checkpoint(span_step), start, pieces)
    return outputs.reshape(length, INNER)


def mixer_part(active, step_sizes, gate_in, head_params, gate_gain, segments):
    values = active[:, :INNER]
    in_b = active[:, INNER : INNER + STATE]
    out_c = active[:, INNER + STATE :]
    decay_log = -step_sizes * jnp.exp(head_params[1])
    scanned = spanned_scan(values, step_sizes, decay_log, in_b, out_c, segments)
    skip_row = jnp.repeat(head_params[2], HEADDIM)
    result = scanned + skip_row[None, :] * values
    gated = result * jax.nn.silu(gate_in)
    return gated * lax.rsqrt(jnp.mean(gated * gated, axis=-1, keepdims=True) + EPS) * gate_gain


def orthogonal(matrix):
    columns = []
    for index in range(matrix.shape[1]):
        vector = matrix[:, index]
        for done in columns:
            vector = vector - jnp.sum(done * vector) * done
        vector = vector * lax.rsqrt(jnp.sum(vector * vector) + GS_EPS)
        columns.append(vector)
    return jnp.stack(columns, axis=1)


def contract_rows(left_mat, right_mat, precision_kind):
    return lax.dot_general(
        left_mat,
        right_mat,
        (((0,), (0,)), ((), ())),
        precision=precision_kind,
        preferred_element_type=jnp.float32,
    )


def plain_update(grad_sum, moment, master, replicas):
    moment_new = MOMENTUM * moment + grad_sum / replicas
    return (moment_new, master - RATE * moment_new)


def on_device(
    tokens,
    segment_ids,
    cotangent,
    in_proj_master,
    out_proj_master,
    in_proj_error,
    out_proj_error,
    in_proj_moment,
    out_proj_moment,
    in_proj_start,
    out_proj_start,
    conv_master,
    conv_moment,
    head_master,
    head_moment,
    norm_gain,
    norm_gain_moment,
    gate_gain,
    gate_gain_moment,
):
    replicas = lax.axis_size("rep")
    w_in, w_out = (
        lax.all_gather(in_proj_master.astype(jnp.bfloat16), "grp", axis=0, tiled=True),
        lax.all_gather(out_proj_master.astype(jnp.bfloat16), "grp", axis=0, tiled=True),
    )
    seq_count, seq_len, width = tokens.shape
    row_count = seq_count * seq_len
    inputs = tokens.astype(jnp.float32)
    normed, norm_back = jax.vjp(prenorm, inputs, norm_gain)
    normed_low = normed.astype(jnp.bfloat16).reshape(row_count, width)
    projected = jnp.dot(normed_low, w_in, preferred_element_type=jnp.float32).reshape(
        seq_count, seq_len, -1
    )

    def first_part(proj_all, conv_params, head_params):
        return jax.vmap(conv_part, in_axes=(0, None, None, 0))(
            proj_all, conv_params, head_params, segment_ids
        )

    (gate_in, active, step_sizes), first_back = jax.vjp(
        first_part, projected, conv_master, head_master
    )
    active_low = lax.optimization_barrier(active.astype(jnp.bfloat16)).astype(jnp.float32)

    def second_part(active_all, sizes_all, gates_all, head_params, out_gain):
        return jax.vmap(mixer_part, in_axes=(0, 0, 0, None, None, 0))(
            active_all, sizes_all, gates_all, head_params, out_gain, segment_ids
        )

    mixed, second_back = jax.vjp(
        second_part, active_low, step_sizes, gate_in, head_master, gate_gain
    )
    mixed_low = mixed.astype(jnp.bfloat16).reshape(row_count, INNER)
    branch = jnp.dot(mixed_low, w_out, preferred_element_type=jnp.float32)
    output = (inputs + branch.reshape(tokens.shape)).astype(jnp.bfloat16)
    cot_rows = cotangent.reshape(row_count, width)
    d_mixed = lax.dot_general(
        cot_rows, w_out, (((1,), (1,)), ((), ())), preferred_element_type=jnp.float32
    )
    out_local = contract_rows(mixed_low, cot_rows, None)
    d_active, d_sizes, d_gates, d_heads_two, d_gate_gain = second_back(d_mixed.reshape(mixed.shape))
    d_projected, d_conv, d_heads_one = first_back((d_gates, d_active, d_sizes))
    d_proj_low = d_projected.astype(jnp.bfloat16).reshape(row_count, -1)
    in_local = contract_rows(normed_low, d_proj_low, None)
    d_normed = lax.dot_general(
        d_proj_low, w_in, (((1,), (1,)), ((), ())), preferred_element_type=jnp.float32
    )
    d_inputs, d_norm_gain = norm_back(d_normed.reshape(normed.shape))
    input_grad = cotangent.astype(jnp.float32) + d_inputs
    in_shard, out_shard = (
        lax.psum_scatter(in_local, "grp", scatter_dimension=0, tiled=True),
        lax.psum_scatter(out_local, "grp", scatter_dimension=0, tiled=True),
    )
    d_heads = d_heads_one + d_heads_two
    whole_in = in_shard + in_proj_error[0]
    whole_out = out_shard + out_proj_error[0]
    left_in = jnp.dot(whole_in, in_proj_start[0], precision=HIGH)
    left_out = jnp.dot(whole_out, out_proj_start[0], precision=HIGH)
    conv_grad, head_grad, norm_gain_grad, gate_gain_grad = lax.psum(
        (d_conv, d_heads, d_norm_gain, d_gate_gain), ("grp", "rep")
    )
    left_in, left_out = lax.psum((left_in, left_out), "rep")
    hat_in = orthogonal(left_in)
    hat_out = orthogonal(left_out)
    right_in = contract_rows(whole_in, hat_in, HIGH)
    right_out = contract_rows(whole_out, hat_out, HIGH)
    right_in, right_out = lax.psum((right_in, right_out), "rep")
    right_in = right_in / replicas
    right_out = right_out / replicas
    approx_in = jnp.dot(hat_in, right_in.T, precision=HIGH)
    approx_out = jnp.dot(hat_out, right_out.T, precision=HIGH)
    in_mom = MOMENTUM * in_proj_moment + approx_in
    out_mom = MOMENTUM * out_proj_moment + approx_out
    in_new = in_proj_master - RATE * in_mom
    out_new = out_proj_master - RATE * out_mom
    conv_mom, conv_new = plain_update(conv_grad, conv_moment, conv_master, replicas)
    head_mom, head_new = plain_update(head_grad, head_moment, head_master, replicas)
    gain_mom, gain_new = plain_update(norm_gain_grad, norm_gain_moment, norm_gain, replicas)
    gate_mom, gate_new = plain_update(gate_gain_grad, gate_gain_moment, gate_gain, replicas)
    return (
        output,
        input_grad,
        in_shard[None],
        out_shard[None],
        hat_in,
        hat_out,
        right_in[None],
        right_out[None],
        (whole_in - approx_in)[None],
        (whole_out - approx_out)[None],
        in_mom,
        out_mom,
        in_new,
        out_new,
        conv_grad,
        conv_mom,
        conv_new,
        head_grad,
        head_mom,
        head_new,
        norm_gain_grad,
        gain_mom,
        gain_new,
        gate_gain_grad,
        gate_mom,
        gate_new,
    )


def solution(mesh):
    return jax.shard_map(
        on_device,
        mesh=mesh,
        in_specs=(
            P(("grp", "rep"), None, None),
            P(("grp", "rep"), None),
            P(("grp", "rep"), None, None),
            P("grp", None),
            P("grp", None),
            P("rep", "grp", None),
            P("rep", "grp", None),
            P("grp", None),
            P("grp", None),
            P("grp", None, None),
            P("grp", None, None),
            P(),
            P(),
            P(),
            P(),
            P(),
            P(),
            P(),
            P(),
        ),
        out_specs=(
            P(("grp", "rep"), None, None),
            P(("grp", "rep"), None, None),
            P("rep", "grp", None),
            P("rep", "grp", None),
            P("grp", None),
            P("grp", None),
            P("grp", None, None),
            P("grp", None, None),
            P("rep", "grp", None),
            P("rep", "grp", None),
            P("grp", None),
            P("grp", None),
            P("grp", None),
            P("grp", None),
            P(),
            P(),
            P(),
            P(),
            P(),
            P(),
            P(),
            P(),
            P(),
            P(),
            P(),
            P(),
        ),
        check_vma=False,
    )
```

profile of v0, /device:TPU:0, one launch (start us, length us, event | category | flops | bytes accessed | tf_op | source)
XLA Modules:
  0.0 1407.3 jit_solution(13596165531728517373)
XLA Ops:
  14.2 39.9 %all-gather.3.cloned.1.call-done = bf16[768,3352]{1,0:T(8,128)(2,1)} async-done(((bf16[192,3352]{1,0:T(8,128)(2,1)}), bf16[768,3352]{1,0:T(8,128)(2,1)}) %all-gather.3.cloned.1.call-update) | async-done | bytes 5148688 | tf_op jit(solution)/shard_map/all_gather | solution.py:148
  75.4 15.0 %multiply_convert_fusion = (bf16[1,1024,1792]{1,2,0:T(8,128)(2,1)S(1)}, f32[1,1024,1792]{1,2,0:T(8,128)}) fusion(f32[1024]{0:T(1024)S(1)} %bitcast.693, f32[1,1021,1792]{1,2,0:T(8,128)} %slice.251, f32[1792]{0:T(1024)S(1)} %get-tuple-element.791, f32[1024]{0:T(1024)S(1)} %bitcast.691, f32[1,1022,1792]{1,2,0:T(8,128)} %slice.250, ...), kind=kLoop, calls=%fused_computation.159 | loop fusion | flops 29360128 | bytes 40375296 | tf_op jit(solution)/shard_map/convert_element_type | solution.py:168
  108.7 254.1 %while.46 = (s32[]{:T(128)}, f32[1,24,64,128]{3,2,1,0:T(8,128)S(1)}, s32[1]{0:T(128)}, f32[4,1,256,1536]{2,0,3,1:T(4,128)}, f32[4,1,24,64,128]{4,3,2,1,0:T(8,128...) while((s32[]{:T(128)}, ...), condition=%wide.region_4.5_spmd.clone, body=%wide.region_1.4_spmd.clone.sunk | while | flops 2527624192 | bytes 27957864 | solution.py:83
  137.4 34.2 %dynamic_update_slice.88 = f32[4,1,256,1536]{2,0,3,1:T(4,128)} dynamic-update-slice(f32[4,1,256,1536]{2,0,3,1:T(4,128)} %get-tuple-element.1300, f32[1,1,256,1536]{2,0,3,1:T(1,128)S(1)} %copy.412, s32[]{:T(128)S(6)} %copy.447, s32[]{:T(128)} %constant.161.clone.1..sunk, s32[]{:T(128)} %constant.161.clone.1..sunk, s32[]{:T(128)} %constant.161.clone.1..sunk) | dynamic-update-slice | bytes 3145732 | tf_op jit(solution)/shard_map/jvp(vmap())/while/body/jit(dynamic_update_index_in_dim)/dynamic_update_slice | solution.py:83
  200.9 34.2 %dynamic_update_slice.88 = f32[4,1,256,1536]{2,0,3,1:T(4,128)} dynamic-update-slice(f32[4,1,256,1536]{2,0,3,1:T(4,128)} %get-tuple-element.1300, f32[1,1,256,1536]{2,0,3,1:T(1,128)S(1)} %copy.412, s32[]{:T(128)S(6)} %copy.447, s32[]{:T(128)} %constant.161.clone.1..sunk, s32[]{:T(128)} %constant.161.clone.1..sunk, s32[]{:T(128)} %constant.161.clone.1..sunk) | dynamic-update-slice | bytes 3145732 | tf_op jit(solution)/shard_map/jvp(vmap())/while/body/jit(dynamic_update_index_in_dim)/dynamic_update_slice | solution.py:83
  264.5 34.2 %dynamic_update_slice.88 = f32[4,1,256,1536]{2,0,3,1:T(4,128)} dynamic-update-slice(f32[4,1,256,1536]{2,0,3,1:T(4,128)} %get-tuple-element.1300, f32[1,1,256,1536]{2,0,3,1:T(1,128)S(1)} %copy.412, s32[]{:T(128)S(6)} %copy.447, s32[]{:T(128)} %constant.161.clone.1..sunk, s32[]{:T(128)} %constant.161.clone.1..sunk, s32[]{:T(128)} %constant.161.clone.1..sunk) | dynamic-update-slice | bytes 3145732 | tf_op jit(solution)/shard_map/jvp(vmap())/while/body/jit(dynamic_update_index_in_dim)/dynamic_update_slice | solution.py:83
  328.0 34.2 %dynamic_update_slice.88 = f32[4,1,256,1536]{2,0,3,1:T(4,128)} dynamic-update-slice(f32[4,1,256,1536]{2,0,3,1:T(4,128)} %get-tuple-element.1300, f32[1,1,256,1536]{2,0,3,1:T(1,128)S(1)} %copy.412, s32[]{:T(128)S(6)} %copy.447, s32[]{:T(128)} %constant.161.clone.1..sunk, s32[]{:T(128)} %constant.161.clone.1..sunk, s32[]{:T(128)} %constant.161.clone.1..sunk) | dynamic-update-slice | bytes 3145732 | tf_op jit(solution)/shard_map/jvp(vmap())/while/body/jit(dynamic_update_index_in_dim)/dynamic_update_slice | solution.py:83
  401.2 19.5 %multiply_reduce_fusion.8 = (f32[1536]{0:T(1024)}, f32[1,1024,1536]{1,2,0:T(8,128)}, f32[1,1024,1536]{1,2,0:T(8,128)}) fusion(f32[1,1024,1792]{1,2,0:T(8,128)} %convert_element_type.87, f32[1,1024,3352]{1,2,0:T(8,128)} %copy-done.1, f32[1,1024,1536]{1,2,0:T(8,128)} %copy-done.7, f32[1024]{0:T(1024)S(1)} %multiply_multiply_fusion.1, f32[1024]{0:T(1024)S(1)} %fusion.124, ...), kind=kLoop, calls=%fused_computation.170 | loop fusion | flops 33028608 | bytes 44066816 | tf_op jit(solution)/shard_map/transpose(jvp(vmap()))/reduce_sum | solution.py:94
  435.3 512.2 %while.47 = (s32[]{:T(128)}, f32[1,24,64,128]{3,2,1,0:T(8,128)S(1)}, f32[4,1,256,1536]{2,0,3,1:T(4,128)}, f32[4,1,24,256]{2,3,1,0:T(8,128)}, f32[4,1,24,256]{3,0...) while((s32[]{:T(128)}, ...), condition=%wide.region_20.21_spmd.clone, body=%wide.region_7.20_spmd.clone.sunk | while | flops 5775293440 | bytes 58667620 | solution.py:83
  529.3 34.1 %dynamic_update_slice.92 = f32[4,1,256,1536]{2,0,3,1:T(4,128)} dynamic-update-slice(f32[4,1,256,1536]{2,0,3,1:T(4,128)} %get-tuple-element.1349, f32[1,1,256,1536]{2,0,3,1:T(1,128)S(1)} %copy.427, s32[]{:T(128)S(6)} %sub.1200, s32[]{:T(128)} %constant.161.clone.1..sunk.1, s32[]{:T(128)} %constant.161.clone.1..sunk.1, s32[]{:T(128)} %constant.161.clone.1..sunk.1) | dynamic-update-slice | bytes 3145732 | tf_op jit(solution)/shard_map/transpose(jvp(vmap()))/while/body/jit(dynamic_update_index_in_dim)/dynamic_update_slice | solution.py:83
  598.9 12.0 fusion.249
  657.3 34.1 %dynamic_update_slice.92 = f32[4,1,256,1536]{2,0,3,1:T(4,128)} dynamic-update-slice(f32[4,1,256,1536]{2,0,3,1:T(4,128)} %get-tuple-element.1349, f32[1,1,256,1536]{2,0,3,1:T(1,128)S(1)} %copy.427, s32[]{:T(128)S(6)} %sub.1200, s32[]{:T(128)} %constant.161.clone.1..sunk.1, s32[]{:T(128)} %constant.161.clone.1..sunk.1, s32[]{:T(128)} %constant.161.clone.1..sunk.1) | dynamic-update-slice | bytes 3145732 | tf_op jit(solution)/shard_map/transpose(jvp(vmap()))/while/body/jit(dynamic_update_index_in_dim)/dynamic_update_slice | solution.py:83
  785.2 34.1 %dynamic_update_slice.92 = f32[4,1,256,1536]{2,0,3,1:T(4,128)} dynamic-update-slice(f32[4,1,256,1536]{2,0,3,1:T(4,128)} %get-tuple-element.1349, f32[1,1,256,1536]{2,0,3,1:T(1,128)S(1)} %copy.427, s32[]{:T(128)S(6)} %sub.1200, s32[]{:T(128)} %constant.161.clone.1..sunk.1, s32[]{:T(128)} %constant.161.clone.1..sunk.1, s32[]{:T(128)} %constant.161.clone.1..sunk.1) | dynamic-update-slice | bytes 3145732 | tf_op jit(solution)/shard_map/transpose(jvp(vmap()))/while/body/jit(dynamic_update_index_in_dim)/dynamic_update_slice | solution.py:83
  913.1 34.1 %dynamic_update_slice.92 = f32[4,1,256,1536]{2,0,3,1:T(4,128)} dynamic-update-slice(f32[4,1,256,1536]{2,0,3,1:T(4,128)} %get-tuple-element.1349, f32[1,1,256,1536]{2,0,3,1:T(1,128)S(1)} %copy.427, s32[]{:T(128)S(6)} %sub.1200, s32[]{:T(128)} %constant.161.clone.1..sunk.1, s32[]{:T(128)} %constant.161.clone.1..sunk.1, s32[]{:T(128)} %constant.161.clone.1..sunk.1) | dynamic-update-slice | bytes 3145732 | tf_op jit(solution)/shard_map/transpose(jvp(vmap()))/while/body/jit(dynamic_update_index_in_dim)/dynamic_update_slice | solution.py:83
  969.8 13.0 multiply_reduce_fusion.7
  1013.7 14.6 %multiply_reduce_fusion.4 = (f32[1792]{0:T(1024)S(1)}, f32[1792]{0:T(1024)S(1)}, f32[1,1024,1792]{1,2,0:T(8,128)}) fusion(f32[1,1024,1792]{1,2,0:T(8,128)S(1)} %bitcast.641, f32[1,1024,3352]{1,2,0:T(8,128)} %copy-done.1, f32[1792]{0:T(1024)S(1)} %copy-done.34, f32[1,1023,1792]{1,2,0:T(8,128)} %slice_multiply_fusion, ...), kind=kLoop, calls=%fused_computation.154 | loop fusion | flops 12841472 | bytes 44018688 | tf_op jit(solution)/shard_map/transpose(jvp(vmap()))/reduce_sum | solution.py:34
  1028.4 15.2 %fusion.107 = f32[768,3352]{1,0:T(8,128)} fusion(bf16[1,1024,768]{2,1,0:T(8,128)(2,1)S(1)} %copy-done.13, f32[768]{0:T(1024)S(1)} %copy-done.50, f32[1024]{0:T(1024)S(1)} %copy-done.52, f32[1,1024,1536]{1,2,0:T(8,128)} %get-tuple-element.1023, f32[1,1024,1792]{1,2,0:T(8,128)} %get-tuple-element.1024, f32[1,1024,24]{1,2,0:T(8,128)S(1)} %get-tuple-element.931), kind=kOutput, calls=%fused_computation.210 | convolution fusion | flops 5285683200 | bytes 25607168 | tf_op jit(solution)/shard_map/dot_general | solution.py:111
  1045.9 14.0 fusion.94
  1059.9 41.2 %all-reduce.25 = (f32[5,1792]{1,0:T(8,128)S(1)}, f32[3,24]{1,0:T(4,128)S(1)}, f32[768]{0:T(1024)S(1)}, f32[1536]{0:T(1024)S(1)}) all-reduce(f32[5,1792]{1,0:T(8,128)S(1)} %pad_add_fusion, f32[3,24]{1,0:T(4,128)} %add_add_fusion.2, f32[768]{0:T(1024)} %get-tuple-element.785, ...), channel_id=1, replica_groups=mesh['grp'=4,'rep'=8] {'grp','rep'}, use_global_device_ids=true, to_apply=%region_105.106 | all-reduce | flops 11336 | bytes 90688 | tf_op jit(solution)/shard_map/psum | solution.py:204
  1120.3 37.0 %psum.57 = f32[384,8]{0,1:T(8,128)S(1)} all-reduce(f32[384,8]{0,1:T(8,128)S(1)} %fusion.118), channel_id=1, replica_groups=mesh['grp'=4,'rep'=8] {'rep'}, use_global_device_ids=true, to_apply=%region_61.62 | all-reduce | flops 3072 | bytes 24576 | tf_op jit(solution)/shard_map/psum | solution.py:207
  1200.7 17.7 %subtract_multiply_fusion.2 = (f32[384,1]{0,1:T(1,128)S(1)}, f32[384,1]{0,1:T(1,128)S(1)}, f32[384,1]{0,1:T(1,128)S(1)}, f32[384,1]{0,1:T(1,128)S(1)}, f32[384,1...) fusion(f32[384,1]{0,1:T(1,128)S(1)} %get-tuple-element.1004, f32[384,8]{0,1:T(8,128)S(1)} %psum.57, ...), kind=kLoop, calls=%fused_computation.318 | loop fusion | flops 24192 | bytes 23180 | tf_op jit(solution)/shard_map/mul | solution.py:105
  1224.9 33.4 %all-reduce.26 = (f32[192,8]{0,1:T(8,128)S(1)}, f32[768,8]{0,1:T(8,128)S(1)}) all-reduce(f32[192,8]{0,1:T(8,128)S(1)} %fusion.110, f32[768,8]{0,1:T(8,128)S(1)} %fusion.128), channel_id=1, replica_groups=mesh['grp'=4,'rep'=8] {'rep'}, use_global_device_ids=true, to_apply=%region_24.25 | all-reduce | flops 7680 | bytes 61440 | tf_op jit(solution)/shard_map/psum | solution.py:207
  1300.2 17.6 %subtract_multiply_fusion.9 = (f32[192,1]{0,1:T(1,128)S(1)}, f32[192,1]{0,1:T(1,128)S(1)}, f32[192,1]{0,1:T(1,128)S(1)}, f32[192,1]{0,1:T(1,128)S(1)}, f32[192,1...) fusion(f32[192,1]{0,1:T(1,128)S(1)} %get-tuple-element.1033, f32[]{:T(128)S(6)} %rsqrt.79, ...), kind=kLoop, calls=%fused_computation.331 | loop fusion | flops 12096 | bytes 11660 | tf_op jit(solution)/shard_map/mul | solution.py:105
  1328.1 61.1 %all-reduce.29.cloned.1.call-done = f32[3352,8]{0,1:T(8,128)} async-done(((f32[3352,8]{0,1:T(8,128)}), f32[3352,8]{0,1:T(8,128)}) %all-reduce.29.cloned.1.call-update) | async-done | bytes 107280 | tf_op jit(solution)/shard_map/psum | solution.py:212
  (693 shorter events, 744.7 us)
Async XLA Ops:
  7.2 1213.6 %copy-start = (f32[1,3352,8]{1,2,0:T(8,128)S(1)}, f32[1,3352,8]{1,2,0:T(8,128)}, u32[]{:S(2)}) copy-start(f32[1,3352,8]{1,2,0:T(8,128)} %param.32) | copy-start | bytes 321796
  7.3 46.8 %all-gather.3.cloned.1.call-start = ((), (), s32[]{:S(2)}) async-start(), calls=%async_computation.2 | async-start | bytes 6635520 | tf_op jit(solution)/shard_map/all_gather | solution.py:148
  10.4 382.1 %all-gather.5.cloned.1.call-start = ((), (), s32[]{:S(2)}) async-start(), calls=%async_computation.3 | async-start | bytes 2949120 | tf_op jit(solution)/shard_map/all_gather | solution.py:149
  12.6 1104.8 %reduce-scatter.5.cloned.1.call-start = ((), (), s32[]{:S(2)}) async-start(), calls=%async_computation.5 | async-start | bytes 5898240 | tf_op jit(solution)/shard_map/reduce_scatter | solution.py:197
  12.8 81.5 %copy-start.58 = (f32[24]{0:T(128)}, f32[24]{0:T(128)S(1)}, u32[]{:S(2)}) copy-start(f32[24]{0:T(128)S(1)} %get-tuple-element.1044) | copy-start | bytes 292
  12.8 81.5 %copy-start.60 = (f32[24]{0:T(128)}, f32[24]{0:T(128)S(1)}, u32[]{:S(2)}) copy-start(f32[24]{0:T(128)S(1)} %get-tuple-element.1045) | copy-start | bytes 292
  13.9 387.3 %copy-start.23 = (f32[1536]{0:T(1024)}, f32[1536]{0:T(1024)S(1)}, u32[]{:S(2)}) copy-start(f32[1536]{0:T(1024)S(1)} %mul.2216) | copy-start | bytes 18436
  14.0 61.4 %copy-start.27 = (f32[1792]{0:T(1024)}, f32[1792]{0:T(1024)S(1)}, u32[]{:S(2)}) copy-start(f32[1792]{0:T(1024)S(1)} %get-tuple-element.791) | copy-start | bytes 21508
  14.0 61.4 %copy-start.29 = (f32[1792]{0:T(1024)}, f32[1792]{0:T(1024)S(1)}, u32[]{:S(2)}) copy-start(f32[1792]{0:T(1024)S(1)} %get-tuple-element.789) | copy-start | bytes 21508
  14.0 61.4 %copy-start.31 = (f32[1792]{0:T(1024)}, f32[1792]{0:T(1024)S(1)}, u32[]{:S(2)}) copy-start(f32[1792]{0:T(1024)S(1)} %get-tuple-element.788) | copy-start | bytes 21508
  14.0 61.4 %copy-start.33 = (f32[1792]{0:T(1024)}, f32[1792]{0:T(1024)S(1)}, u32[]{:S(2)}) copy-start(f32[1792]{0:T(1024)S(1)} %get-tuple-element.790) | copy-start | bytes 21508
  14.1 61.2 %copy-start.37 = (f32[1,1024]{1,0:T(1,128)}, f32[1,1024]{1,0:T(1,128)S(1)}, u32[]{:S(2)}) copy-start(f32[1,1024]{1,0:T(1,128)S(1)} %get-tuple-element.1040) | copy-start | bytes 12292
  14.1 61.2 %copy-start.39 = (f32[1,1024]{1,0:T(1,128)}, f32[1,1024]{1,0:T(1,128)S(1)}, u32[]{:S(2)}) copy-start(f32[1,1024]{1,0:T(1,128)S(1)} %get-tuple-element.1041) | copy-start | bytes 12292
  14.2 61.2 %copy-start.43 = (f32[1,1024]{1,0:T(1,128)}, f32[1,1024]{1,0:T(1,128)S(1)}, u32[]{:S(2)}) copy-start(f32[1,1024]{1,0:T(1,128)S(1)} %get-tuple-element.1042) | copy-start | bytes 12292
  401.1 819.6 %reduce-scatter.3.cloned.1.call-start = ((), (), s32[]{:S(2)}) async-start(), calls=%async_computation.4 | async-start | bytes 13271040 | tf_op jit(solution)/shard_map/reduce_scatter | solution.py:196
  1043.6 345.6 %all-reduce.29.cloned.1.call-start = ((), (), s32[]{:S(2)}) async-start(), calls=%async_computation.6 | async-start | bytes 221184 | tf_op jit(solution)/shard_map/psum | solution.py:212
  1045.8 58.8 %copy-start.46 = (f32[1536]{0:T(1024)S(1)}, f32[1536]{0:T(1024)}, u32[]{:S(2)}) copy-start(f32[1536]{0:T(1024)} %param.40) | copy-start | bytes 18436
  1045.8 58.8 %copy-start.55 = (f32[1536]{0:T(1024)S(1)}, f32[1536]{0:T(1024)}, u32[]{:S(2)}) copy-start(f32[1536]{0:T(1024)} %param.41) | copy-start | bytes 18436
  1045.9 59.4 %copy-start.22 = (f32[5,1792]{1,0:T(8,128)S(1)}, f32[5,1792]{1,0:T(8,128)}, u32[]{:S(2)}) copy-start(f32[5,1792]{1,0:T(8,128)} %param.34) | copy-start | bytes 107524
  1045.9 59.4 %copy-start.35 = (f32[5,1792]{1,0:T(8,128)S(1)}, f32[5,1792]{1,0:T(8,128)}, u32[]{:S(2)}) copy-start(f32[5,1792]{1,0:T(8,128)} %param.35) | copy-start | bytes 107524
  1045.9 60.0 %copy-start.15 = (bf16[1,1024,768]{2,1,0:T(8,128)(2,1)S(1)}, bf16[1,1024,768]{2,1,0:T(8,128)(2,1)}, u32[]{:S(2)}) copy-start(bf16[1,1024,768]{2,1,0:T(8,128)(2,1)} %param.25) | copy-start | bytes 4718596
  1117.4 103.4 %copy-start.8 = (f32[1,192,3352]{2,1,0:T(8,128)S(1)}, f32[1,192,3352]{2,1,0:T(8,128)}, u32[]{:S(2)}) copy-start(f32[1,192,3352]{2,1,0:T(8,128)} %param.28) | copy-start | bytes 7723012
  1218.4 103.5 %copy-start.25 = (f32[384,8]{0,1:T(8,128)}, f32[384,8]{0,1:T(8,128)S(1)}, u32[]{:S(2)}) copy-start(f32[384,8]{0,1:T(8,128)S(1)} %stack.5) | copy-start | bytes 36868
  1317.8 72.9 %copy-start.26 = (f32[192,8]{0,1:T(8,128)}, f32[192,8]{0,1:T(8,128)S(1)}, u32[]{:S(2)}) copy-start(f32[192,8]{0,1:T(8,128)S(1)} %stack.4) | copy-start | bytes 18436
  (72 other events, 918.0 us)
Sparse Core Ops, SparseCore 0:
  10.5 43.4 all-gather.2
  56.2 24.0 all-gather.4
  401.3 47.9 reduce-scatter.4
  1043.7 85.9 reduce-scatter.2
  1322.0 67.0 all-reduce.28
where the time goes:
time: 1430 us; the launch traced here: 1410 us
  local copies, waits for them, and re-layouts  541 us (38%)
  other arithmetic  333 us (23%)
  matrix products  282 us (20%)
  blocking collectives  112 us (8%)
  waiting for transfers between devices  101 us (7%)
  between operations  25.8 us (2%)
    dynamic_update_slice x32, local copies, waits for them, and re-layouts, spanned_scan(): ended, outputs = lax.scan(jax.checkpoint(span_step), start, pieces)  352 us
    dot_general x12, matrix products, span_step(): local_out = jnp.einsum('hij,jhp->ihp', mixing, heads_vals, precision=HIGH)  107 us
    psum x2, blocking collectives, on_device(): left_in, left_out = lax.psum((left_in, left_out), 'rep')  70.4 us
    psum x1, waiting for transfers between devices, on_device(): right_in, right_out = lax.psum((right_in, right_out), 'rep')  61.1 us
    reduce_sum x20, other arithmetic, orthogonal(): vector = vector - jnp.sum(done * vector) * done  58.9 us
    psum x1, blocking collectives, on_device(): lax.psum((d_conv, d_heads, d_norm_gain, d_gate_gain), ('grp', 'rep'))  41.2 us
    all_gather x1, waiting for transfers between devices, on_device(): lax.all_gather(in_proj_master.astype(jnp.bfloat16), 'grp', axis=0, tiled=...  39.9 us
    dot_general x16, matrix products, span_step(): carried = jnp.einsum('in,hpn->ihp', out_c, state, precision=HIGH)  39.5 us
  transfers between devices with their start and end apart: 5, of which 2 were waited for; matrix products, arithmetic and copies ran while one was open for 76% of the time, Pallas kernels for 0%

commit v1 on v0

v1 whole, which is shorter than its diff:
```python
import jax
import jax.numpy as jnp
from jax import lax
from jax.experimental import pallas as pl
from jax.experimental.pallas import tpu as pltpu
from jax.sharding import PartitionSpec as P

HEADS = 24
HEADDIM = 64
STATE = 128
CONV = 4
INNER = 1536
CONVDIM = 1792
Q = 128
EPS = 1e-05
GS_EPS = 1e-06
MOMENTUM = 0.9
RATE = 0.01
LOG2E = 1.4426950408889634
F32 = jnp.float32
BF16 = jnp.bfloat16
VMEM_LIMIT = 60 * 1024 * 1024


def mm(a, b):
    return lax.dot_general(a, b, (((1,), (0,)), ((), ())), preferred_element_type=F32)


def mm_nt(a, b):
    return lax.dot_general(a, b, (((1,), (1,)), ((), ())), preferred_element_type=F32)


def split2(v):
    high = v.astype(BF16)
    return high, (v - high.astype(F32)).astype(BF16)


def split3(v):
    high = v.astype(BF16)
    rest = v - high.astype(F32)
    middle = rest.astype(BF16)
    return high, middle, (rest - middle.astype(F32)).astype(BF16)


def mm_two(a, exact):
    high, rest = split2(a)
    return mm(high, exact) + mm(rest, exact)


def mm_exact_left(exact, b):
    high, middle, rest = split3(b)
    return mm(exact, high) + mm(exact, middle) + mm(exact, rest)


def mm_three(a, b):
    a_high, a_rest = split2(a)
    b_high, b_rest = split2(b)
    return mm(a_high, b_high) + mm(a_high, b_rest) + mm(a_rest, b_high)


def sigmoid(v):
    return 0.5 * jnp.tanh(0.5 * v) + 0.5


def softplus(v):
    return jnp.maximum(v, 0.0) + jnp.log1p(jnp.exp(-jnp.abs(v)))


def whole_spec(array):
    rank = len(array.shape)
    return pl.BlockSpec(array.shape, lambda i, *_: (0,) * rank)


def row_spec(rows, cols, order=None):
    return pl.BlockSpec((rows, cols), (lambda i, *_: (i, 0)) if order is None else order)


ANY = pl.BlockSpec(memory_space=pl.ANY)
SMEM = pl.BlockSpec(memory_space=pltpu.SMEM)


def params():
    return pltpu.CompilerParams(dimension_semantics=("arbitrary",), vmem_limit_bytes=VMEM_LIMIT)


def fetch(place, pieces, buffer, sems):
    copies = []
    for index, piece in enumerate(pieces):
        copies.append(
            pltpu.make_async_copy(piece, buffer.at[jnp.bitwise_xor(place, index)], sems.at[index])
        )
    for copy in copies:
        copy.start()
    for copy in copies:
        copy.wait()


def forward_kernel(count, place, x_ref, aux_ref, segr_ref, gain_ref, conv_ref, head_ref, tri_ref, spread_ref, *rest):
    pieces = rest[:count]
    normed_ref, cin_ref, dsilu_ref, active_ref, y_ref, v_ref, cum_ref, states_ref = rest[count : count + 8]
    weights, conv_buf, state, sems = rest[count + 8 :]
    step = pl.program_id(0)

    @pl.when(step == 0)
    def _():
        fetch(place[0], pieces, weights, sems)
        conv_buf[0:8, :] = jnp.zeros((8, CONVDIM), F32)
        state[...] = jnp.zeros_like(state)

    @pl.when(step > 0)
    def _():
        conv_buf[0:8, :] = conv_buf[Q : Q + 8, :]

    x = x_ref[...].astype(F32)
    inv = lax.rsqrt(jnp.mean(x * x, axis=-1, keepdims=True) + EPS)
    normed = (x * inv * gain_ref[...]).astype(BF16)
    normed_ref[...] = normed
    weight = weights[...].reshape(weights.shape[0] * weights.shape[1], weights.shape[2])
    projected = mm(normed, weight)
    cin_ref[...] = projected[:, :CONVDIM].astype(BF16)
    conv_buf[8 : 8 + Q, :] = projected[:, :CONVDIM]
    total = conv_ref[CONV : CONV + 1, :] + conv_ref[CONV - 1 : CONV, :] * conv_buf[8 : 8 + Q, :]
    for k in range(1, CONV):
        total = total + conv_ref[CONV - 1 - k : CONV - k, :] * (conv_buf[8 - k : 8 - k + Q, :] * aux_ref[:, k : k + 1])
    gate = sigmoid(total)
    active = (total * gate).astype(BF16)
    active_ref[...] = active
    dsilu_ref[...] = (gate * (1.0 + total * (1.0 - gate))).astype(BF16)

    v = projected[:, CONVDIM : CONVDIM + HEADS] + head_ref[0:1, :HEADS]
    v_ref[...] = v
    sizes = softplus(v)
    decay_log = -sizes * jnp.exp(head_ref[1:2, :HEADS])
    cum = mm_exact_left(tri_ref[...], decay_log)
    cum_ref[...] = cum
    spread = spread_ref[...]
    alive = aux_ref[:, 7:8]
    tail = jnp.exp(cum[Q - 1 : Q, :] - cum) * aux_ref[:, 8:9] * sizes
    sizes_wide = mm_two(sizes, spread)
    alive_wide = mm_two(jnp.exp(cum) * alive, spread)
    tail_wide = mm_two(tail, spread)
    values = active[:, :INNER].astype(F32)
    in_b = active[:, INNER : INNER + STATE]
    out_c = active[:, INNER + STATE :]
    sized = (values * sizes_wide).astype(BF16)
    tailed = (values * tail_wide).astype(BF16)

    states_ref[0] = state[...].astype(BF16)
    carried = mm(out_c, state[...].astype(BF16)) * alive_wide
    state[...] = state[...] * alive_wide[Q - 1 : Q, :] + mm(in_b.astype(F32).T.astype(BF16), tailed)

    rows = lax.broadcasted_iota(jnp.int32, (Q, Q), 0)
    cols = lax.broadcasted_iota(jnp.int32, (Q, Q), 1)
    allowed = (rows >= cols) & (aux_ref[:, 0:1] == segr_ref[0])
    inner = jnp.where(allowed, mm_nt(out_c, in_b), 0.0)
    scaled = cum * LOG2E
    scaled_t = jnp.concatenate([scaled, jnp.zeros((Q, Q - HEADS), F32)], axis=1).T
    left_half = lax.broadcasted_iota(jnp.int32, (Q, 2 * HEADDIM), 1) < HEADDIM
    zero = jnp.zeros((Q, 2 * HEADDIM), BF16)
    for pair in range(HEADS // 2):
        mixes = []
        for h in (2 * pair, 2 * pair + 1):
            gap = jnp.minimum(scaled[:, h : h + 1] - scaled_t[h : h + 1, :], 0.0)
            mixes.append((inner * jnp.exp2(gap)).astype(BF16))
        block = sized[:, pair * 128 : pair * 128 + 128]
        both = jnp.concatenate([jnp.where(left_half, block, zero), jnp.where(left_half, zero, block)], axis=0)
        local = mm(jnp.concatenate(mixes, axis=1), both)
        y_ref[:, pair * 128 : pair * 128 + 128] = (local + carried[:, pair * 128 : pair * 128 + 128]).astype(BF16)


def forward_call(place, x, aux, segr, gain, conv, head, tri, spread, pieces):
    length, width = x.shape
    steps = length // Q
    count = len(pieces)
    cols = pieces[0].shape[1]
    outs = (
        jax.ShapeDtypeStruct((length, width), BF16),
        jax.ShapeDtypeStruct((length, CONVDIM), BF16),
        jax.ShapeDtypeStruct((length, CONVDIM), BF16),
        jax.ShapeDtypeStruct((length, CONVDIM), BF16),
        jax.ShapeDtypeStruct((length, INNER), BF16),
        jax.ShapeDtypeStruct((length, HEADS), F32),
        jax.ShapeDtypeStruct((length, HEADS), F32),
        jax.ShapeDtypeStruct((steps, STATE, INNER), BF16),
    )

    def kernel(*refs):
        forward_kernel(count, *refs)

    return pl.pallas_call(
        kernel,
        grid=(steps,),
        in_specs=[
            SMEM,
            row_spec(Q, width),
            row_spec(Q, aux.shape[1]),
            pl.BlockSpec((1, 1, Q), lambda i: (i, 0, 0)),
            whole_spec(gain),
            whole_spec(conv),
            whole_spec(head),
            whole_spec(tri),
            whole_spec(spread),
        ]
        + [ANY] * count,
        out_specs=[
            row_spec(Q, width),
            row_spec(Q, CONVDIM),
            row_spec(Q, CONVDIM),
            row_spec(Q, CONVDIM),
            row_spec(Q, INNER),
            row_spec(Q, HEADS),
            row_spec(Q, HEADS),
            pl.BlockSpec((1, STATE, INNER), lambda i: (i, 0, 0)),
        ],
        out_shape=outs,
        scratch_shapes=[
            pltpu.VMEM((count,) + pieces[0].shape, BF16),
            pltpu.VMEM((Q + 8, CONVDIM), F32),
            pltpu.VMEM((STATE, INNER), F32),
            pltpu.SemaphoreType.DMA((count,)),
        ],
        compiler_params=params(),
        name="forward_scan",
    )(place, x, aux, segr, gain, conv, head, tri, spread, *pieces)


def gate_kernel(count, place, normed_ref, y_ref, values_ref, x_ref, cot_ref, skip_ref, gain_ref, *rest):
    gate_pieces = rest[:count]
    out_pieces = rest[count : 2 * count]
    output_ref, mixed_ref, dgate_ref, dres_ref, sums_ref = rest[2 * count : 2 * count + 5]
    gate_w, out_w, sems = rest[2 * count + 5 :]
    step = pl.program_id(0)

    @pl.when(step == 0)
    def _():
        fetch(place[0], gate_pieces, gate_w, sems)
        fetch(place[0], out_pieces, out_w, sems)
        sums_ref[...] = jnp.zeros_like(sums_ref)

    gate_weight = gate_w[...].reshape(gate_w.shape[0] * gate_w.shape[1], gate_w.shape[2])
    out_weight = out_w[...].reshape(out_w.shape[0] * out_w.shape[1], out_w.shape[2])
    gate_in = mm(normed_ref[...], gate_weight)
    d_mixed = mm_nt(cot_ref[...], out_weight)
    gain = gain_ref[...]
    values = values_ref[...].astype(F32)
    result = y_ref[...].astype(F32) + skip_ref[...] * values
    sig = sigmoid(gate_in)
    silu = gate_in * sig
    gated = result * silu
    inv = lax.rsqrt(jnp.mean(gated * gated, axis=-1, keepdims=True) + EPS)
    unit = gated * inv
    mixed = (unit * gain).astype(BF16)
    mixed_ref[...] = mixed
    output_ref[...] = (x_ref[...].astype(F32) + mm(mixed, out_weight)).astype(BF16)
    product = d_mixed * unit
    d_unit = d_mixed * gain
    d_gated = inv * (d_unit - unit * jnp.mean(product * gain, axis=-1, keepdims=True))
    d_result = d_gated * silu
    dgate_ref[...] = (d_gated * result * (sig * (1.0 + gate_in * (1.0 - sig)))).astype(BF16)
    dres_ref[...] = d_result.astype(BF16)
    sums_ref[0:1, :] += jnp.sum(product, axis=0, keepdims=True)
    sums_ref[1:2, :] += jnp.sum(d_result * values, axis=0, keepdims=True)


def gate_call(place, normed, y, active, x, cot, skip, gain, gate_pieces, out_pieces, rows):
    length, width = x.shape
    count = len(gate_pieces)

    def kernel(*refs):
        gate_kernel(count, *refs)

    return pl.pallas_call(
        kernel,
        grid=(length // rows,),
        in_specs=[
            SMEM,
            row_spec(rows, width),
            row_spec(rows, INNER),
            row_spec(rows, INNER),
            row_spec(rows, width),
            row_spec(rows, width),
            whole_spec(skip),
            whole_spec(gain),
        ]
        + [ANY] * (2 * count),
        out_specs=[
            row_spec(rows, width),
            row_spec(rows, INNER),
            row_spec(rows, INNER),
            row_spec(rows, INNER),
            pl.BlockSpec((8, INNER), lambda i: (0, 0)),
        ],
        out_shape=(
            jax.ShapeDtypeStruct((length, width), BF16),
            jax.ShapeDtypeStruct((length, INNER), BF16),
            jax.ShapeDtypeStruct((length, INNER), BF16),
            jax.ShapeDtypeStruct((length, INNER), BF16),
            jax.ShapeDtypeStruct((8, INNER), F32),
        ),
        scratch_shapes=[
            pltpu.VMEM((count,) + gate_pieces[0].shape, BF16),
            pltpu.VMEM((count,) + out_pieces[0].shape, BF16),
            pltpu.SemaphoreType.DMA((count,)),
        ],
        compiler_params=params(),
        name="gate_both_ways",
    )(place, normed, y, active, x, cot, skip, gain, *gate_pieces, *out_pieces)


def backward_kernel(
    dy_ref, active_ref, cin_ref, dsilu_ref, v_ref, cum_ref, states_ref, aux_ref, segr_ref, conv_ref, head_ref, skip_ref,
    triu_ref, spread_ref, gather_ref, dproj_ref, dconv_ref, dhead_ref, conv_buf, dstate
):
    step = pl.program_id(0)

    @pl.when(step == 0)
    def _():
        conv_buf[...] = jnp.zeros_like(conv_buf)
        dstate[...] = jnp.zeros_like(dstate)
        dconv_ref[...] = jnp.zeros_like(dconv_ref)
        dhead_ref[...] = jnp.zeros_like(dhead_ref)

    @pl.when(step > 0)
    def _():
        conv_buf[Q : Q + 8, :] = conv_buf[0:8, :]

    spread = spread_ref[...]
    gather = gather_ref[...]
    dy = dy_ref[...]
    dy_wide = dy.astype(F32)
    values = active_ref[:, :INNER].astype(F32)
    in_b = active_ref[:, INNER : INNER + STATE]
    out_c = active_ref[:, INNER + STATE :]
    v = v_ref[...]
    cum = cum_ref[...]
    sizes = softplus(v)
    rate = jnp.exp(head_ref[1:2, :HEADS])
    alive_wide = mm_two(jnp.exp(cum) * aux_ref[:, 7:8], spread)
    tail_wide = mm_two(jnp.exp(cum[Q - 1 : Q, :] - cum) * aux_ref[:, 8:9], spread)
    sizes_wide = mm_two(sizes, spread)
    sized = (values * sizes_wide).astype(BF16)
    sized_wide = sized.astype(F32)
    entry = states_ref[0]
    grad_state = dstate[...]
    grad_low = grad_state.astype(BF16)

    carried = mm(out_c, entry) * alive_wide
    dy_alive = (dy_wide * alive_wide).astype(BF16)
    d_c = mm_nt(dy_alive, entry)
    tailed = (sized_wide * tail_wide).astype(BF16)
    d_b = mm_nt(tailed, grad_low)
    d_sized_far = mm(in_b, grad_low) * tail_wide
    keep = alive_wide[Q - 1 : Q, :]
    end_part = jnp.sum(grad_state * entry.astype(F32), axis=0, keepdims=True) * keep
    end_part = end_part + jnp.sum(sized_wide * d_sized_far, axis=0, keepdims=True)
    dstate[...] = grad_state * keep + mm(out_c.astype(F32).T.astype(BF16), dy_alive)

    rows = lax.broadcasted_iota(jnp.int32, (Q, Q), 0)
    cols = lax.broadcasted_iota(jnp.int32, (Q, Q), 1)
    allowed = (cols >= rows) & (aux_ref[:, 0:1] == segr_ref[0])
    inner = jnp.where(allowed, mm_nt(in_b, out_c), 0.0)
    scaled = cum * LOG2E
    scaled_t = jnp.concatenate([scaled, jnp.zeros((Q, Q - HEADS), F32)], axis=1).T
    left_half = lax.broadcasted_iota(jnp.int32, (Q, 2 * HEADDIM), 1) < HEADDIM
    zero = jnp.zeros((Q, 2 * HEADDIM), BF16)
    d_inner = jnp.zeros((Q, Q), F32)
    row_sums = []
    near = []
    for pair in range(HEADS // 2):
        lanes = slice(pair * 128, pair * 128 + 128)
        dy_block = dy[:, lanes]
        dy_both = jnp.concatenate(
            [jnp.where(left_half, dy_block, zero), jnp.where(left_half, zero, dy_block)], axis=0
        )
        d_mix = mm_nt(sized[:, lanes], dy_both)
        mixes = []
        for side in range(2):
            h = 2 * pair + side
            gap = jnp.minimum(scaled_t[h : h + 1, :] - scaled[:, h : h + 1], 0.0)
            decay = jnp.exp2(gap)
            mix = (inner * decay).astype(BF16)
            d_one = d_mix[:, side * Q : side * Q + Q]
            d_inner = d_inner + d_one * decay
            row_sums.append(jnp.sum(d_one * mix.astype(F32), axis=0, keepdims=True))
            mixes.append(mix)
        near.append(mm(jnp.concatenate(mixes, axis=1), dy_both))
    d_sized = jnp.concatenate(near, axis=1) + d_sized_far
    d_inner = jnp.where(allowed, d_inner, 0.0)
    d_inner_low = d_inner.astype(BF16)
    d_b = d_b + mm(d_inner_low, out_c)
    d_c = d_c + mm(d_inner.T.astype(BF16), in_b)

    row_part = jnp.concatenate(row_sums + [jnp.zeros((Q - HEADS, Q), F32)], axis=0).T[:, :HEADS]
    d_cum = row_part + mm_two(dy_wide * carried - sized_wide * d_sized, gather)[:, :HEADS]
    end_sum = mm_two(jnp.broadcast_to(end_part, (8, INNER)), gather)[0:1, :HEADS]
    d_log = mm_exact_left(triu_ref[...], d_cum) + end_sum
    d_steps = mm_two(values * d_sized, gather)[:, :HEADS] - rate * d_log
    d_v = d_steps * sigmoid(v)
    dhead_ref[0:1, :HEADS] += jnp.sum(d_v, axis=0, keepdims=True)
    dhead_ref[1:2, :HEADS] += jnp.sum(d_log * (-sizes * rate), axis=0, keepdims=True)
    dproj_ref[:, CONVDIM : CONVDIM + HEADS] = d_v.astype(BF16)

    d_values = d_sized * sizes_wide + skip_ref[...] * dy_wide
    conv_buf[0:Q, :INNER] = d_values * dsilu_ref[:, :INNER].astype(F32)
    conv_buf[0:Q, INNER : INNER + STATE] = d_b * dsilu_ref[:, INNER : INNER + STATE].astype(F32)
    conv_buf[0:Q, INNER + STATE :] = d_c * dsilu_ref[:, INNER + STATE :].astype(F32)
    cin = cin_ref[...].astype(F32)
    first = conv_buf[0:Q, :]
    total = first * conv_ref[CONV - 1 : CONV, :]
    dconv_ref[CONV : CONV + 1, :] += jnp.sum(first, axis=0, keepdims=True)
    dconv_ref[CONV - 1 : CONV, :] += jnp.sum(first * cin, axis=0, keepdims=True)
    for k in range(1, CONV):
        moved = conv_buf[k : k + Q, :] * aux_ref[:, 3 + k : 4 + k]
        total = total + moved * conv_ref[CONV - 1 - k : CONV - k, :]
        dconv_ref[CONV - 1 - k : CONV - k, :] += jnp.sum(moved * cin, axis=0, keepdims=True)
    dproj_ref[:, :CONVDIM] = total.astype(BF16)


def backward_call(dy, active, cin, dsilu, v, cum, states, aux, segr, conv, head, skip, triu, spread, gather):
    length = dy.shape[0]
    steps = length // Q

    def back(i):
        return (steps - 1 - i, 0)

    def back3(i):
        return (steps - 1 - i, 0, 0)

    return pl.pallas_call(
        backward_kernel,
        grid=(steps,),
        in_specs=[
            row_spec(Q, INNER, back),
            row_spec(Q, CONVDIM, back),
            row_spec(Q, CONVDIM, back),
            row_spec(Q, CONVDIM, back),
            row_spec(Q, HEADS, back),
            row_spec(Q, HEADS, back),
            pl.BlockSpec((1, STATE, INNER), back3),
            row_spec(Q, aux.shape[1], back),
            pl.BlockSpec((1, 1, Q), back3),
            whole_spec(conv),
            whole_spec(head),
            whole_spec(skip),
            whole_spec(triu),
            whole_spec(spread),
            whole_spec(gather),
        ],
        out_specs=[
            row_spec(Q, CONVDIM + HEADS, back),
            pl.BlockSpec((8, CONVDIM), lambda i: (0, 0)),
            pl.BlockSpec((8, 128), lambda i: (0, 0)),
        ],
        out_shape=(
            jax.ShapeDtypeStruct((length, CONVDIM + HEADS), BF16),
            jax.ShapeDtypeStruct((8, CONVDIM), F32),
            jax.ShapeDtypeStruct((8, 128), F32),
        ),
        scratch_shapes=[pltpu.VMEM((Q + 8, CONVDIM), F32), pltpu.VMEM((STATE, INNER), F32)],
        compiler_params=params(),
        name="backward_scan",
    )(dy, active, cin, dsilu, v, cum, states, aux, segr, conv, head, skip, triu, spread, gather)


def input_kernel(count, place, dgate_ref, dproj_ref, x_ref, cot_ref, gain_ref, *rest):
    gate_pieces = rest[:count]
    conv_pieces = rest[count : 2 * count]
    grad_ref, sums_ref = rest[2 * count : 2 * count + 2]
    gate_w, conv_w, sems = rest[2 * count + 2 :]
    step = pl.program_id(0)

    @pl.when(step == 0)
    def _():
        fetch(place[0], gate_pieces, gate_w, sems)
        fetch(place[0], conv_pieces, conv_w, sems)
        sums_ref[...] = jnp.zeros_like(sums_ref)

    gate_weight = gate_w[...].reshape(gate_w.shape[0] * gate_w.shape[1], gate_w.shape[2])
    conv_weight = conv_w[...].reshape(conv_w.shape[0] * conv_w.shape[1], conv_w.shape[2])
    d_normed = mm_nt(dgate_ref[...], gate_weight) + mm_nt(dproj_ref[...], conv_weight)
    x = x_ref[...].astype(F32)
    inv = lax.rsqrt(jnp.mean(x * x, axis=-1, keepdims=True) + EPS)
    unit = x * inv
    product = d_normed * unit
    gain = gain_ref[...]
    sums_ref[0:1, :] += jnp.sum(product, axis=0, keepdims=True)
    grad = inv * (d_normed * gain - unit * jnp.mean(product * gain, axis=-1, keepdims=True))
    grad_ref[...] = cot_ref[...].astype(F32) + grad


def input_call(place, dgate, dproj, x, cot, gain, gate_pieces, conv_pieces, rows):
    length, width = x.shape
    count = len(gate_pieces)

    def kernel(*refs):
        input_kernel(count, *refs)

    return pl.pallas_call(
        kernel,
        grid=(length // rows,),
        in_specs=[
            SMEM,
            row_spec(rows, dgate.shape[1]),
            row_spec(rows, dproj.shape[1]),
            row_spec(rows, width),
            row_spec(rows, width),
            whole_spec(gain),
        ]
        + [ANY] * (2 * count),
        out_specs=[row_spec(rows, width), pl.BlockSpec((8, width), lambda i: (0, 0))],
        out_shape=(jax.ShapeDtypeStruct((length, width), F32), jax.ShapeDtypeStruct((8, width), F32)),
        scratch_shapes=[
            pltpu.VMEM((count,) + gate_pieces[0].shape, BF16),
            pltpu.VMEM((count,) + conv_pieces[0].shape, BF16),
            pltpu.SemaphoreType.DMA((count,)),
        ],
        compiler_params=params(),
        name="input_grad",
    )(place, dgate, dproj, x, cot, gain, *gate_pieces, *conv_pieces)


def left_kernel(
    gate_a, gate_b, conv_a, conv_b, out_a, out_b, err_in, err_out, start_in, start_out,
    grad_in, grad_out, whole_in, whole_out, left_ref
):
    gate = gate_a[...].astype(F32) + gate_b[...].astype(F32)
    conv = conv_a[...].astype(F32) + conv_b[...].astype(F32)
    out = out_a[...].astype(F32) + out_b[...].astype(F32)
    grad_in[:, :INNER] = gate
    grad_in[:, INNER:] = conv
    grad_out[...] = out
    gate = gate + err_in[:, :INNER]
    conv = conv + err_in[:, INNER:]
    out = out + err_out[...]
    whole_in[:, :INNER] = gate
    whole_in[:, INNER:] = conv
    whole_out[...] = out
    left_in = mm_three(gate, start_in[:INNER, :]) + mm_three(conv, start_in[INNER:, :])
    left_out = mm_three(out, start_out[...])
    tall = jnp.concatenate([left_in, left_out], axis=0)
    rank = tall.shape[1]
    tall = jnp.concatenate([tall, jnp.zeros((tall.shape[0], 128 - rank), F32)], axis=1)
    extra = left_ref.shape[1] - tall.shape[0]
    if extra:
        tall = jnp.concatenate([tall, jnp.zeros((extra, 128), F32)], axis=0)
    left_ref[...] = tall.T[:rank, :]


def up(value, unit):
    return -(-value // unit) * unit


def left_call(gate, conv, out, err_in, err_out, start_in, start_out):
    rows_in, cols_in = err_in.shape
    rows_out, cols_out = err_out.shape
    rank = start_in.shape[1]
    shapes = (
        jax.ShapeDtypeStruct((rows_in, cols_in), F32),
        jax.ShapeDtypeStruct((rows_out, cols_out), F32),
        jax.ShapeDtypeStruct((rows_in, cols_in), F32),
        jax.ShapeDtypeStruct((rows_out, cols_out), F32),
        jax.ShapeDtypeStruct((rank, up(rows_in + rows_out, 128)), F32),
    )
    return pl.pallas_call(
        left_kernel,
        out_shape=shapes,
        compiler_params=pltpu.CompilerParams(vmem_limit_bytes=VMEM_LIMIT),
        name="left_factors",
    )(*gate, *conv, *out, err_in, err_out, start_in, start_out)


def gram_schmidt(rows):
    count = rows.shape[0]
    places = lax.broadcasted_iota(jnp.int32, (count, 1), 0)
    for index in range(count):
        one = rows[index : index + 1, :]
        one = one * lax.rsqrt(jnp.sum(one * one, axis=1, keepdims=True) + GS_EPS)
        shares = jnp.sum(rows * one, axis=1, keepdims=True)
        rows = jnp.where(places > index, rows - shares * one, jnp.where(places == index, one, rows))
    return rows


def right_kernel(left_ref, whole_in, whole_out, hat_in, hat_out, right_ref):
    rows_in, cols_in = whole_in.shape
    rows_out, cols_out = whole_out.shape
    rank = left_ref.shape[0]
    left = left_ref[...]
    places = lax.broadcasted_iota(jnp.int32, left.shape, 1)
    both_in = gram_schmidt(jnp.where(places < rows_in, left, 0.0))
    both_out = gram_schmidt(jnp.where((places >= rows_in) & (places < rows_in + rows_out), left, 0.0))
    tall = jnp.concatenate([both_in + both_out, jnp.zeros((128 - rank, left.shape[1]), F32)], axis=0).T
    hat_in[...] = tall[:rows_in, :rank]
    hat_out[...] = tall[rows_in : rows_in + rows_out, :rank]
    right_ref[:, :cols_in] = mm_three(both_in[:, :rows_in], whole_in[...])
    out_rows = both_out[:, rows_in : rows_in + rows_out]
    right_ref[:, up(cols_in, 128) : up(cols_in, 128) + cols_out] = mm_three(out_rows, whole_out[...])


def right_call(left, whole_in, whole_out):
    rank = left.shape[0]
    width = up(whole_in.shape[1], 128) + up(whole_out.shape[1], 128)
    return pl.pallas_call(
        right_kernel,
        out_shape=(
            jax.ShapeDtypeStruct((whole_in.shape[0], rank), F32),
            jax.ShapeDtypeStruct((whole_out.shape[0], rank), F32),
            jax.ShapeDtypeStruct((rank, width), F32),
        ),
        compiler_params=pltpu.CompilerParams(vmem_limit_bytes=VMEM_LIMIT),
        name="right_factors",
    )(left, whole_in, whole_out)


def final_kernel(
    scale, right_ref, hat_in, whole_in, mom_in, mas_in, hat_out, whole_out, mom_out, mas_out,
    right_in_ref, err_in, new_mom_in, new_mas_in, right_out_ref, err_out, new_mom_out, new_mas_out
):
    cols_in = whole_in.shape[1]
    cols_out = whole_out.shape[1]
    skip = up(cols_in, 128)
    rank = right_ref.shape[0]

    @pl.when(pl.program_id(0) == 0)
    def _():
        right = right_ref[...] * scale
        tall = jnp.concatenate([right, jnp.zeros((128 - rank, right.shape[1]), F32)], axis=0).T
        right_in_ref[...] = tall[:cols_in, :rank]
        right_out_ref[...] = tall[skip : skip + cols_out, :rank]

    def one(hat, right, whole, mom, mas, err, new_mom, new_mas):
        approx = mm_three(hat[...], right)
        err[...] = whole[...] - approx
        fresh = MOMENTUM * mom[...] + approx
        new_mom[...] = fresh
        new_mas[...] = mas[...] - RATE * fresh

    one(hat_in, right_ref[:, :cols_in] * scale, whole_in, mom_in, mas_in, err_in, new_mom_in, new_mas_in)
    one(
        hat_out, right_ref[:, skip : skip + cols_out] * scale, whole_out, mom_out, mas_out, err_out, new_mom_out, new_mas_out
    )


def final_call(scale, right, hat_in, whole_in, mom_in, mas_in, hat_out, whole_out, mom_out, mas_out, blocks):
    rank = right.shape[0]

    def kernel(*refs):
        final_kernel(scale, *refs)

    def specs(rows, cols):
        return [row_spec(rows // blocks, rank)] + [row_spec(rows // blocks, cols)] * 3

    def out_specs(rows, cols):
        return [pl.BlockSpec((cols, rank), lambda i: (0, 0))] + [row_spec(rows // blocks, cols)] * 3

    def shapes(rows, cols):
        return [jax.ShapeDtypeStruct((cols, rank), F32)] + [jax.ShapeDtypeStruct((rows, cols), F32)] * 3

    size_in, size_out = whole_in.shape, whole_out.shape
    return pl.pallas_call(
        kernel,
        grid=(blocks,),
        in_specs=[whole_spec(right)] + specs(*size_in) + specs(*size_out),
        out_specs=out_specs(*size_in) + out_specs(*size_out),
        out_shape=shapes(*size_in) + shapes(*size_out),
        compiler_params=params(),
        name="final_update",
    )(right, hat_in, whole_in, mom_in, mas_in, hat_out, whole_out, mom_out, mas_out)


def flip(value, axis, bit):
    size = lax.axis_size(axis)
    return lax.ppermute(value, axis, [(i, i ^ bit) for i in range(size)])


def bits_of(axis):
    size = lax.axis_size(axis)
    assert size & (size - 1) == 0
    return [1 << k for k in range(size.bit_length() - 1)]


def gather_pieces(shard, axis):
    pieces = {0: shard}
    for bit in reversed(bits_of(axis)):
        for index in sorted(pieces):
            pieces[index | bit] = flip(pieces[index], axis, bit)
    return [pieces[index] for index in range(len(pieces))]


def scatter_pieces(whole, axis):
    size = lax.axis_size(axis)
    place = lax.axis_index(axis)
    rows = whole.shape[0] // size
    pieces = {
        index: lax.dynamic_slice_in_dim(whole, jnp.bitwise_xor(place, index) * rows, rows, 0) for index in range(size)
    }
    bits = bits_of(axis)
    for bit in bits:
        arrived = {index: flip(pieces[index | bit], axis, bit) for index in sorted(pieces) if not index & bit}
        if bit == bits[-1]:
            return pieces[0], arrived[0]
        pieces = {
            index: (pieces[index].astype(F32) + arrived[index].astype(F32)).astype(BF16) for index in arrived
        }


def sum_all(value, axis):
    for bit in bits_of(axis):
        value = value + flip(value, axis, bit)
    return value


def rows_product(left, right):
    return lax.dot_general(left, right, (((0,), (0,)), ((), ())), preferred_element_type=F32).astype(BF16)


def plain_update(grad_sum, moment, master, replicas):
    moment_new = MOMENTUM * moment + grad_sum / replicas
    return (moment_new, master - RATE * moment_new)


def position_table(ids):
    length = ids.shape[0]
    places = jnp.arange(length)
    columns = [ids.astype(F32)]
    for k in range(1, CONV):
        earlier = jnp.concatenate([jnp.full((k,), -1, ids.dtype), ids[:-k]])
        columns.append((earlier == ids).astype(F32))
    for k in range(1, CONV):
        later = jnp.concatenate([ids[k:], jnp.full((k,), -1, ids.dtype)])
        columns.append((later == ids).astype(F32))
    ends = ids.reshape(length // Q, Q)[:, -1]
    before = jnp.concatenate([jnp.full((1,), -1, ids.dtype), ends[:-1]])
    columns.append((jnp.repeat(before, Q) == ids).astype(F32))
    columns.append((jnp.repeat(ends, Q) == ids).astype(F32))
    columns.append(places.astype(F32) * 0.0)
    return jnp.stack(columns, axis=1)


def on_device(
    tokens,
    segment_ids,
    cotangent,
    in_proj_master,
    out_proj_master,
    in_proj_error,
    out_proj_error,
    in_proj_moment,
    out_proj_moment,
    in_proj_start,
    out_proj_start,
    conv_master,
    conv_moment,
    head_master,
    head_moment,
    norm_gain,
    norm_gain_moment,
    gate_gain,
    gate_gain_moment,
):
    replicas = lax.axis_size("rep")
    x = tokens[0]
    cot = cotangent[0]
    length, width = x.shape
    place = lax.axis_index("grp").astype(jnp.int32).reshape(1)
    conv_w = gather_pieces(in_proj_master[:, INNER:].astype(BF16), "grp")
    gate_w = gather_pieces(in_proj_master[:, :INNER].astype(BF16), "grp")
    out_w = gather_pieces(out_proj_master.astype(BF16), "grp")

    aux = position_table(segment_ids[0])
    segr = segment_ids[0].astype(F32).reshape(length // Q, 1, Q)
    conv = jnp.pad(conv_master, ((0, 3), (0, 0)))
    head = jnp.pad(head_master, ((0, 5), (0, 128 - HEADS)))
    skip = jnp.repeat(head_master[2], HEADDIM)[None]
    lanes = jnp.arange(INNER) // HEADDIM
    spread = (jnp.arange(HEADS)[:, None] == lanes[None, :]).astype(BF16)
    gather = (lanes[:, None] == jnp.arange(128)[None, :]).astype(BF16)
    order = jnp.arange(Q)
    tri = (order[:, None] >= order[None, :]).astype(BF16)
    triu = (order[:, None] <= order[None, :]).astype(BF16)

    normed, cin, dsilu, active, y, v, cum, states = forward_call(
        place, x, aux, segr, norm_gain[None], conv, head, tri, spread, conv_w
    )
    output, mixed, d_gate, d_result, gate_sums = gate_call(
        place, normed, y, active, x, cot, skip, gate_gain[None], gate_w, out_w, 256
    )
    out_pair = scatter_pieces(rows_product(mixed, cot), "grp")
    gate_pair = scatter_pieces(rows_product(normed, d_gate), "grp")
    d_proj, conv_sums, head_sums = backward_call(
        d_result, active, cin, dsilu, v, cum, states, aux, segr, conv, head, skip, triu, spread, gather
    )
    conv_pair = scatter_pieces(rows_product(normed, d_proj), "grp")
    input_grad, norm_sums = input_call(place, d_gate, d_proj, x, cot, norm_gain[None], gate_w, conv_w, 256)

    skip_grad = jnp.sum(gate_sums[1].reshape(HEADS, HEADDIM), axis=1)
    small = jnp.concatenate(
        [
            conv_sums[: CONV + 1].reshape(-1),
            head_sums[0, :HEADS],
            head_sums[1, :HEADS],
            skip_grad,
            norm_sums[0],
            gate_sums[0],
        ]
    )
    count = small.shape[0]
    small = jnp.pad(small, (0, up(count, 1024) - count)).reshape(-1, 128)
    small = sum_all(sum_all(small, "grp"), "rep").reshape(-1)
    sizes = [(CONV + 1) * CONVDIM, 3 * HEADS, width, INNER]
    parts = []
    begin = 0
    for size in sizes:
        parts.append(small[begin : begin + size])
        begin += size
    conv_grad = parts[0].reshape(CONV + 1, CONVDIM)
    head_grad = parts[1].reshape(3, HEADS)
    norm_gain_grad, gate_gain_grad = parts[2], parts[3]

    in_shard, out_shard, whole_in, whole_out, left = left_call(
        gate_pair, conv_pair, out_pair, in_proj_error[0], out_proj_error[0], in_proj_start[0], out_proj_start[0]
    )
    left = sum_all(left, "rep")
    hat_in, hat_out, right = right_call(left, whole_in, whole_out)
    right = sum_all(right, "rep")
    right_in, in_err, in_mom, in_new, right_out, out_err, out_mom, out_new = final_call(
        1.0 / replicas, right, hat_in, whole_in, in_proj_moment, in_proj_master,
        hat_out, whole_out, out_proj_moment, out_proj_master, 4,
    )
    conv_mom, conv_new = plain_update(conv_grad, conv_moment, conv_master, replicas)
    head_mom, head_new = plain_update(head_grad, head_moment, head_master, replicas)
    gain_mom, gain_new = plain_update(norm_gain_grad, norm_gain_moment, norm_gain, replicas)
    gate_mom, gate_new = plain_update(gate_gain_grad, gate_gain_moment, gate_gain, replicas)
    return (
        output[None],
        input_grad[None],
        in_shard[None],
        out_shard[None],
        hat_in,
        hat_out,
        right_in[None],
        right_out[None],
        in_err[None],
        out_err[None],
        in_mom,
        out_mom,
        in_new,
        out_new,
        conv_grad,
        conv_mom,
        conv_new,
        head_grad,
        head_mom,
        head_new,
        norm_gain_grad,
        gain_mom,
        gain_new,
        gate_gain_grad,
        gate_mom,
        gate_new,
    )


def solution(mesh):
    return jax.shard_map(
        on_device,
        mesh=mesh,
        in_specs=(
            P(("grp", "rep"), None, None),
            P(("grp", "rep"), None),
            P(("grp", "rep"), None, None),
            P("grp", None),
            P("grp", None),
            P("rep", "grp", None),
            P("rep", "grp", None),
            P("grp", None),
            P("grp", None),
            P("grp", None, None),
            P("grp", None, None),
            P(),
            P(),
            P(),
            P(),
            P(),
            P(),
            P(),
            P(),
        ),
        out_specs=(
            P(("grp", "rep"), None, None),
            P(("grp", "rep"), None, None),
            P("rep", "grp", None),
            P("rep", "grp", None),
            P("grp", None),
            P("grp", None),
            P("grp", None, None),
            P("grp", None, None),
            P("rep", "grp", None),
            P("rep", "grp", None),
            P("grp", None),
            P("grp", None),
            P("grp", None),
            P("grp", None),
            P(),
            P(),
            P(),
            P(),
            P(),
            P(),
            P(),
            P(),
            P(),
            P(),
            P(),
            P(),
        ),
        check_vma=False,
    )
```

time: 1430 us -> 299 us (0.21); the launches traced: 1410 us -> 298 us
  local copies, waits for them, and re-layouts: 541 us -> 25.6 us
  other arithmetic: 333 us -> 18.9 us
  matrix products: 282 us -> 12.4 us
  Pallas kernels: 0 us -> 120 us
  blocking collectives: 112 us -> 0 us
  between operations: 25.8 us -> 1.08 us
  starting transfers between devices: 0.21 us -> 24.1 us
    dynamic_update_slice x32 -> x0, local copies, waits for them, and re-layouts: 352 us -> none  [spanned_scan(): ended, outputs = lax.scan(jax.checkpoint(span_step), start, pieces)]
    dot_general x68 -> x3, matrix products: 282 us -> 12.4 us  [rows_product(): lax.dot_general(left, right, (((0,), (0,)), ((), ())), preferred_element_...]
    reduce_sum x45 -> x1, other arithmetic: 149 us -> 0.12 us  [on_device(): skip_grad = jnp.sum(gate_sums[1].reshape(HEADS, HEADDIM), axis=1)]
    pallas_call x0 -> x7, Pallas kernels: none -> 120 us  [the longest x1 40.3 us: backward_call(): pl.pallas_call(backward_kernel, grid=(steps,), in_specs=[row_spec(Q, INNE...]
    psum x3 -> x0, blocking collectives: 112 us -> none  [the longest x2 70.4 us: on_device(): left_in, left_out = lax.psum((left_in, left_out), 'rep')]
    ppermute x0 -> x29, waiting for transfers between devices: none -> 96.2 us  [flip(): return lax.ppermute(value, axis, [(i, i ^ bit) for i in range(size)])]
    mul x49 -> x1, other arithmetic: 92 us -> 0.01 us  [position_table(): columns.append(places.astype(F32) * 0.0)]
    psum x1 -> x0, waiting for transfers between devices: 61.1 us -> none  [on_device(): right_in, right_out = lax.psum((right_in, right_out), 'rep')]
  transfers between devices with their start and end apart: 5 -> 29, of which waited for: 2 -> 12; matrix products, arithmetic and copies ran while one was open for 76% -> 12% of each run, Pallas kernels for 0% -> 15%
where the time goes in v1:
time: 299 us; the launch traced here: 298 us
  Pallas kernels  120 us (40%)
  waiting for transfers between devices  96.2 us (32%)
  local copies, waits for them, and re-layouts  25.6 us (9%)
  starting transfers between devices  24.1 us (8%)
  other arithmetic  18.9 us (6%)
  matrix products  12.4 us (4%)
    ppermute x29, waiting for transfers between devices, flip(): return lax.ppermute(value, axis, [(i, i ^ bit) for i in range(size)])  96.2 us
    pallas_call x1, Pallas kernels, backward_call(): pl.pallas_call(backward_kernel, grid=(steps,), in_specs=[row_spec(Q, INNE...  40.3 us
    ppermute x29, starting transfers between devices, flip(): return lax.ppermute(value, axis, [(i, i ^ bit) for i in range(size)])  24.1 us
    pallas_call x1, Pallas kernels, forward_call(): pl.pallas_call(kernel, grid=(steps,), in_specs=[SMEM, row_spec(Q, width),...  23.8 us
    pallas_call x1, Pallas kernels, gate_call(): pl.pallas_call(kernel, grid=(length // rows,), in_specs=[SMEM, row_spec(r...  17.7 us
    unnamed x70, local copies, waits for them, and re-layouts  15.7 us
    pallas_call x1, Pallas kernels, input_call(): pl.pallas_call(kernel, grid=(length // rows,), in_specs=[SMEM, row_spec(r...  14 us
    dot_general x3, matrix products, rows_product(): lax.dot_general(left, right, (((0,), (0,)), ((), ())), preferred_element_...  12.4 us
  transfers between devices with their start and end apart: 29, of which 12 were waited for; matrix products, arithmetic and copies ran while one was open for 12% of the time, Pallas kernels for 15%

profile of v1, /device:TPU:0, one launch (start us, length us, event | category | flops | bytes accessed | tf_op | source)
XLA Modules:
  0.0 298.2 jit_solution(17489208896950614729)
XLA Ops:
  2.8 3.1 %collective-permute-start.1 = (bf16[192,1816]{1,0:T(8,128)(2,1)S(1)}, bf16[192,1816]{1,0:T(8,128)(2,1)S(1)}, u32[]{:S(2)}, u32[]{:S(2)}) collective-permute-start(bf16[192,1816]{1,0:T(8,128)(2,1)S(1)} %slice.110.refs_9_.refs_10_), channel_id=1, source_target_pairs={{0,16},{8,24},{16,0},{24,8},{1,17},{9,25},{17,1},{25,9},{2,18},{10... | collective-permute-start | bytes 2092040 | tf_op jit(solution)/shard_map/ppermute | solution.py:672
  11.3 11.9 %collective-permute-done.1.refs_11_.refs_12_ = bf16[192,1816]{1,0:T(8,128)(2,1)S(1)} collective-permute-done((bf16[192,1816]{1,0:T(8,128)(2,1)S(1)}, bf16[192,1816]{1,0:T(8,128)(2,1)S(1)}, u32[]{:S(2)}, u32[]{:S(2)}) %collective-permute-start.1) | collective-permute-done | bytes 697376 | tf_op jit(solution)/shard_map/ppermute | solution.py:672
  23.9 12.1 %collective-permute-done.4.refs_10_.refs_8_ = bf16[192,1536]{1,0:T(8,128)(2,1)} collective-permute-done((bf16[192,1536]{1,0:T(8,128)(2,1)S(1)}, bf16[192,1536]{1,0:T(8,128)(2,1)}, u32[]{:S(2)}, u32[]{:S(2)}) %collective-permute-start.4) | collective-permute-done | bytes 589856 | tf_op jit(solution)/shard_map/ppermute | solution.py:672
  36.0 11.8 %collective-permute-done.7.refs_14_ = bf16[384,768]{1,0:T(8,128)(2,1)} collective-permute-done((bf16[384,768]{1,0:T(8,128)(2,1)}, bf16[384,768]{1,0:T(8,128)(2,1)}, u32[]{:S(2)}, u32[]{:S(2)}) %collective-permute-start.7) | collective-permute-done | bytes 589856 | tf_op jit(solution)/shard_map/ppermute | solution.py:672
  55.0 23.8 %forward_scan.1 = (bf16[1024,768]{1,0:T(8,128)(2,1)}, bf16[1024,1792]{1,0:T(8,128)(2,1)}, bf16[1024,1792]{1,0:T(8,128)(2,1)}, bf16[1024,1792]{1,0:T(8,128)(2,1)}...) custom-call(s32[1]{0:T(128)} %bitcast.refs_0_, ...), custom_call_target="tpu_custom_call" | custom-call | tf_op jit(solution)/shard_map/forward_scan/pallas_call | solution.py:190
  78.9 17.7 %gate_both_ways.1 = (bf16[1024,768]{1,0:T(8,128)(2,1)}, bf16[1024,1536]{1,0:T(8,128)(2,1)}, bf16[1024,1536]{1,0:T(8,128)(2,1)}, bf16[1024,1536]{1,0:T(8,128)(2,1)}, f32[8,1536]{1,0:T(8,128)}) custom-call(s32[1]{0:T(128)} %bitcast.refs_0_, bf16[1024,768]{1,0:T(8,128)(2,1)} %get-tuple-element.60.refs_1_, bf16[1024,1536]{1,0:T(8,128)(2,1)} %get-tuple-element.61.refs_2_, ...), custom_call_target="tpu_custom_call" | custom-call | tf_op jit(solution)/shard_map/gate_both_ways/pallas_call | solution.py:272
  96.6 40.3 %backward_scan.1 = (bf16[1024,1816]{1,0:T(8,128)(2,1)}, f32[8,1792]{1,0:T(8,128)}, f32[8,128]{1,0:T(8,128)}) custom-call(bf16[1024,1536]{1,0:T(8,128)(2,1)} %get-tuple-element.65.dy_ref, bf16[1024,1792]{1,0:T(8,128)(2,1)} %get-tuple-element.62.refs_3_.active_ref, bf16[1024,1792]{1,0:T(8,128)(2,1)} %get-tuple-element.66.cin_ref, ...), custom_call_target="tpu_custom_call" | custom-call | tf_op jit(solution)/shard_map/backward_scan/pallas_call | solution.py:429
  137.7 4.7 %convolution_convert_fusion = bf16[1536,768]{1,0:T(8,128)(2,1)S(1)} fusion(bf16[1024,1536]{1,0:T(8,128)(2,1)} %get-tuple-element.73, bf16[1,1024,768]{2,1,0:T(8,128)(2,1)S(1)} %copy-done.1), kind=kOutput, calls=%fused_computation | convolution fusion | flops 2417098752 | bytes 7077888 | tf_op jit(solution)/shard_map/dot_general | solution.py:713
  145.0 3.7 %convolution_convert_fusion.2 = bf16[768,1816]{1,0:T(8,128)(2,1)S(1)} fusion(bf16[1024,768]{1,0:T(8,128)(2,1)S(1)} %copy-done.13, bf16[1024,1816]{1,0:T(8,128)(2,1)S(1)} %copy-done.4), kind=kOutput, calls=%fused_computation.2 | convolution fusion | flops 2857715712 | bytes 8081408 | tf_op jit(solution)/shard_map/dot_general | solution.py:713
  152.0 3.9 %convolution_convert_fusion.1 = bf16[768,1536]{1,0:T(8,128)(2,1)} fusion(bf16[1024,768]{1,0:T(8,128)(2,1)S(1)} %copy-done.13, bf16[1024,1536]{1,0:T(8,128)(2,1)S(1)} %copy-done.5), kind=kOutput, calls=%fused_computation.1 | convolution fusion | flops 2417098752 | bytes 7077888 | tf_op jit(solution)/shard_map/dot_general | solution.py:713
  156.0 14.0 %input_grad.1 = (f32[1024,768]{1,0:T(8,128)}, f32[8,768]{1,0:T(8,128)}) custom-call(s32[1]{0:T(128)} %bitcast.refs_0_, bf16[1024,1536]{1,0:T(8,128)(2,1)} %get-tuple-element.64.refs_1_, bf16[1024,1816]{1,0:T(8,128)(2,1)} %get-tuple-element.71.refs_2_, bf16[1024,768]{1,0:T(8,128)(2,1)} %bitcast.64, bf16[1024,768]{1,0:T(8,128)(2,1)} %bitcast.67, ...), custom_call_target="tpu_custom_call" | custom-call | tf_op jit(solution)/shard_map/input_grad/pallas_call | solution.py:498
  173.6 2.6 add_convert_fusion.2
  177.9 2.6 add_convert_fusion
  184.2 36.9 %collective-permute-done.25 = f32[96,128]{1,0:T(8,128)S(1)} collective-permute-done((f32[96,128]{1,0:T(8,128)S(1)}, f32[96,128]{1,0:T(8,128)S(1)}, u32[]{:S(2)}, u32[]{:S(2)}) %collective-permute-start.25) | collective-permute-done | bytes 49184 | tf_op jit(solution)/shard_map/ppermute | solution.py:672
  229.5 3.4 %collective-permute-start.28 = (f32[96,128]{1,0:T(8,128)S(1)}, f32[96,128]{1,0:T(8,128)S(1)}, u32[]{:S(2)}, u32[]{:S(2)}) collective-permute-start(f32[96,128]{1,0:T(8,128)S(1)} %add.137), channel_id=1, source_target_pairs={{0,4},{1,5},{2,6},{3,7},{4,0},{5,1},{6,2},{7,3},{8,12},{9,13},{10,... | collective-permute-start | bytes 147464 | tf_op jit(solution)/shard_map/ppermute | solution.py:672
  236.6 8.0 %left_factors.1 = (f32[192,3352]{1,0:T(8,128)}, f32[384,768]{1,0:T(8,128)}, f32[192,3352]{1,0:T(8,128)}, f32[384,768]{1,0:T(8,128)}, f32[8,640]{1,0:T(8,128)}) custom-call(bf16[192,1536]{1,0:T(8,128)(2,1)} %get-tuple-element.193.gate_a, bf16[192,1536]{1,0:T(8,128)(2,1)} %copy-done.15, bf16[192,1816]{1,0:T(8,128)(2,1)} %get-tuple-element.185.conv_a, ...), custom_call_target="tpu_custom_call" | custom-call | tf_op jit(solution)/shard_map/left_factors/pallas_call | solution.py:564
  250.5 2.6 collective-permute-done.19
  253.9 3.9 %collective-permute-done.20 = f32[8,640]{1,0:T(8,128)S(1)} collective-permute-done((f32[8,640]{1,0:T(8,128)S(1)}, f32[8,640]{1,0:T(8,128)S(1)}, u32[]{:S(2)}, u32[]{:S(2)}) %collective-permute-start.20) | collective-permute-done | bytes 20512 | tf_op jit(solution)/shard_map/ppermute | solution.py:672
  258.4 5.2 %right_factors.1 = (f32[192,8]{1,0:T(8,128)}, f32[384,8]{1,0:T(8,128)}, f32[8,4224]{1,0:T(8,128)}) custom-call(f32[8,640]{1,0:T(8,128)} %add.130.left_ref, f32[192,3352]{1,0:T(8,128)} %get-tuple-element.77.whole_in.refs_2_, f32[384,768]{1,0:T(8,128)} %get-tuple-element.78.whole_out.refs_6_), custom_call_target="tpu_custom_call" | custom-call | tf_op jit(solution)/shard_map/right_factors/pallas_call | solution.py:602
  265.7 3.1 %collective-permute-done.21 = f32[8,4224]{1,0:T(8,128)S(1)} collective-permute-done((f32[8,4224]{1,0:T(8,128)}, f32[8,4224]{1,0:T(8,128)S(1)}, u32[]{:S(2)}, u32[]{:S(2)}) %collective-permute-start.21) | collective-permute-done | bytes 135200 | tf_op jit(solution)/shard_map/ppermute | solution.py:672
  271.6 3.3 %collective-permute-done.22 = f32[8,4224]{1,0:T(8,128)S(1)} collective-permute-done((f32[8,4224]{1,0:T(8,128)S(1)}, f32[8,4224]{1,0:T(8,128)S(1)}, u32[]{:S(2)}, u32[]{:S(2)}) %collective-permute-start.22) | collective-permute-done | bytes 135200 | tf_op jit(solution)/shard_map/ppermute | solution.py:672
  278.8 3.5 %collective-permute-done.23 = f32[8,4224]{1,0:T(8,128)S(1)} collective-permute-done((f32[8,4224]{1,0:T(8,128)S(1)}, f32[8,4224]{1,0:T(8,128)S(1)}, u32[]{:S(2)}, u32[]{:S(2)}) %collective-permute-start.23) | collective-permute-done | bytes 135200 | tf_op jit(solution)/shard_map/ppermute | solution.py:672
  283.0 10.9 %final_update.1 = (f32[3352,8]{1,0:T(8,128)}, f32[192,3352]{1,0:T(8,128)}, f32[192,3352]{1,0:T(8,128)}, f32[192,3352]{1,0:T(8,128)}, f32[768,8]{1,0:T(8,128)}, /...) custom-call(f32[8,4224]{1,0:T(8,128)} %add.133.refs_0_, f32[192,8]{1,0:T(8,128)} %get-tuple-element.150.refs_1_, ...), custom_call_target="tpu_custom_call" | custom-call | tf_op jit(solution)/shard_map/final_update/pallas_call | solution.py:659
  293.8 2.6 copy.85
  (177 shorter events, 61.7 us)
Async XLA Ops:
  2.8 20.4 %collective-permute-start.1 = (bf16[192,1816]{1,0:T(8,128)(2,1)S(1)}, bf16[192,1816]{1,0:T(8,128)(2,1)S(1)}, u32[]{:S(2)}, u32[]{:S(2)}) collective-permute-start(bf16[192,1816]{1,0:T(8,128)(2,1)S(1)} %slice.110.refs_9_.refs_10_), channel_id=1, source_target_pairs={{0,16},{8,24},{16,0},{24,8},{1,17},{9,25},{17,1},{25,9},{2,18},{10... | collective-permute-start | bytes 2092040 | tf_op jit(solution)/shard_map/ppermute | solution.py:672
  5.9 41.9 %collective-permute-start = (bf16[192,1816]{1,0:T(8,128)(2,1)S(1)}, bf16[192,1816]{1,0:T(8,128)(2,1)}, u32[]{:S(2)}, u32[]{:S(2)}) collective-permute-start(bf16[192,1816]{1,0:T(8,128)(2,1)S(1)} %slice.110.refs_9_.refs_10_), channel_id=1, source_target_pairs={{0,8},{8,0},{16,24},{24,16},{1,9},{9,1},{17,25},{25,17},{2,10},{10... | collective-permute-start | bytes 2092040 | tf_op jit(solution)/shard_map/ppermute | solution.py:672
  5.9 30.0 %collective-permute-start.4 = (bf16[192,1536]{1,0:T(8,128)(2,1)S(1)}, bf16[192,1536]{1,0:T(8,128)(2,1)}, u32[]{:S(2)}, u32[]{:S(2)}) collective-permute-start(bf16[192,1536]{1,0:T(8,128)(2,1)S(1)} %slice.111.refs_8_.refs_6_), channel_id=1, source_target_pairs={{0,16},{8,24},{16,0},{24,8},{1,17},{9,25},{17,1},{25,9},{2,18},{10... | collective-permute-start | bytes 1769480 | tf_op jit(solution)/shard_map/ppermute | solution.py:672
  6.1 72.8 %collective-permute-start.3 = (bf16[192,1536]{1,0:T(8,128)(2,1)S(1)}, bf16[192,1536]{1,0:T(8,128)(2,1)}, u32[]{:S(2)}, u32[]{:S(2)}) collective-permute-start(bf16[192,1536]{1,0:T(8,128)(2,1)S(1)} %slice.111.refs_8_.refs_6_), channel_id=1, source_target_pairs={{0,8},{8,0},{16,24},{24,16},{1,9},{9,1},{17,25},{25,17},{2,10},{10... | collective-permute-start | bytes 1769480 | tf_op jit(solution)/shard_map/ppermute | solution.py:672
  7.5 40.3 %collective-permute-start.7 = (bf16[384,768]{1,0:T(8,128)(2,1)}, bf16[384,768]{1,0:T(8,128)(2,1)}, u32[]{:S(2)}, u32[]{:S(2)}) collective-permute-start(bf16[384,768]{1,0:T(8,128)(2,1)} %convert_element_type.175.refs_12_), channel_id=1, source_target_pairs={{0,16},{8,24},{16,0},{24,8},{1,17},{9,25},{17,1},{25,9},{2,18},{10... | collective-permute-start | bytes 1769480 | tf_op jit(solution)/shard_map/ppermute | solution.py:672
  23.2 31.0 %collective-permute-start.2 = (bf16[192,1816]{1,0:T(8,128)(2,1)S(1)}, bf16[192,1816]{1,0:T(8,128)(2,1)S(1)}, u32[]{:S(2)}, u32[]{:S(2)}) collective-permute-start(bf16[192,1816]{1,0:T(8,128)(2,1)S(1)} %collective-permute-done.1.refs_11_.refs_12_), channel_id=1, source_target_pairs={{0,8},{8,0},{16,24},{24,16},{1,9},{9,1},{17,25},{25,17},{2,10},{10... | collective-permute-start | bytes 2092040 | tf_op jit(solution)/shard_map/ppermute | solution.py:672
  35.9 42.9 %collective-permute-start.6 = (bf16[384,768]{1,0:T(8,128)(2,1)}, bf16[384,768]{1,0:T(8,128)(2,1)}, u32[]{:S(2)}, u32[]{:S(2)}) collective-permute-start(bf16[384,768]{1,0:T(8,128)(2,1)} %convert_element_type.175.refs_12_), channel_id=1, source_target_pairs={{0,8},{8,0},{16,24},{24,16},{1,9},{9,1},{17,25},{25,17},{2,10},{10... | collective-permute-start | bytes 1769480 | tf_op jit(solution)/shard_map/ppermute | solution.py:672
  47.7 31.2 %collective-permute-start.5 = (bf16[192,1536]{1,0:T(8,128)(2,1)}, bf16[192,1536]{1,0:T(8,128)(2,1)}, u32[]{:S(2)}, u32[]{:S(2)}) collective-permute-start(bf16[192,1536]{1,0:T(8,128)(2,1)} %collective-permute-done.4.refs_10_.refs_8_), channel_id=1, source_target_pairs={{0,8},{8,0},{16,24},{24,16},{1,9},{9,1},{17,25},{25,17},{2,10},{10... | collective-permute-start | bytes 1769480 | tf_op jit(solution)/shard_map/ppermute | solution.py:672
  47.7 31.2 %collective-permute-start.8 = (bf16[384,768]{1,0:T(8,128)(2,1)}, bf16[384,768]{1,0:T(8,128)(2,1)}, u32[]{:S(2)}, u32[]{:S(2)}) collective-permute-start(bf16[384,768]{1,0:T(8,128)(2,1)} %collective-permute-done.7.refs_14_), channel_id=1, source_target_pairs={{0,8},{8,0},{16,24},{24,16},{1,9},{9,1},{17,25},{25,17},{2,10},{10... | collective-permute-start | bytes 1769480 | tf_op jit(solution)/shard_map/ppermute | solution.py:672
  143.5 28.7 %collective-permute-start.15 = (bf16[384,768]{1,0:T(8,128)(2,1)}, bf16[384,768]{1,0:T(8,128)(2,1)}, u32[]{:S(2)}, u32[]{:S(2)}) collective-permute-start(bf16[384,768]{1,0:T(8,128)(2,1)} %get-tuple-element.191), channel_id=1, source_target_pairs={{0,8},{8,0},{16,24},{24,16},{1,9},{9,1},{17,25},{25,17},{2,10},{10... | collective-permute-start | bytes 1769480 | tf_op jit(solution)/shard_map/ppermute | solution.py:672
  143.6 29.1 %collective-permute-start.16 = (bf16[384,768]{1,0:T(8,128)(2,1)}, bf16[384,768]{1,0:T(8,128)(2,1)}, u32[]{:S(2)}, u32[]{:S(2)}) collective-permute-start(bf16[384,768]{1,0:T(8,128)(2,1)} %get-tuple-element.190), channel_id=1, source_target_pairs={{0,8},{8,0},{16,24},{24,16},{1,9},{9,1},{17,25},{25,17},{2,10},{10... | collective-permute-start | bytes 1769480 | tf_op jit(solution)/shard_map/ppermute | solution.py:672
  151.5 24.7 %collective-permute-start.12 = (bf16[192,1816]{1,0:T(8,128)(2,1)}, bf16[192,1816]{1,0:T(8,128)(2,1)S(1)}, u32[]{:S(2)}, u32[]{:S(2)}) collective-permute-start(bf16[192,1816]{1,0:T(8,128)(2,1)} %get-tuple-element.187), channel_id=1, source_target_pairs={{0,8},{8,0},{16,24},{24,16},{1,9},{9,1},{17,25},{25,17},{2,10},{10... | collective-permute-start | bytes 2092040 | tf_op jit(solution)/shard_map/ppermute | solution.py:672
  151.5 26.4 %collective-permute-start.13 = (bf16[192,1816]{1,0:T(8,128)(2,1)}, bf16[192,1816]{1,0:T(8,128)(2,1)}, u32[]{:S(2)}, u32[]{:S(2)}) collective-permute-start(bf16[192,1816]{1,0:T(8,128)(2,1)} %get-tuple-element.186), channel_id=1, source_target_pairs={{0,8},{8,0},{16,24},{24,16},{1,9},{9,1},{17,25},{25,17},{2,10},{10... | collective-permute-start | bytes 2092040 | tf_op jit(solution)/shard_map/ppermute | solution.py:672
  172.0 11.9 %collective-permute-start.24 = (f32[96,128]{1,0:T(8,128)S(1)}, f32[96,128]{1,0:T(8,128)S(1)}, u32[]{:S(2)}, u32[]{:S(2)}) collective-permute-start(f32[96,128]{1,0:T(8,128)S(1)} %pad_bitcast_fusion), channel_id=1, source_target_pairs={{0,8},{8,0},{16,24},{24,16},{1,9},{9,1},{17,25},{25,17},{2,10},{10... | collective-permute-start | bytes 147464 | tf_op jit(solution)/shard_map/ppermute | solution.py:672
  172.2 8.6 %collective-permute-start.10 = (bf16[192,1536]{1,0:T(8,128)(2,1)S(1)}, bf16[192,1536]{1,0:T(8,128)(2,1)S(1)}, u32[]{:S(2)}, u32[]{:S(2)}) collective-permute-start(bf16[192,1536]{1,0:T(8,128)(2,1)S(1)} %get-tuple-element.194), channel_id=1, source_target_pairs={{0,8},{8,0},{16,24},{24,16},{1,9},{9,1},{17,25},{25,17},{2,10},{10... | collective-permute-start | bytes 1769480 | tf_op jit(solution)/shard_map/ppermute | solution.py:672
  172.7 8.1 %collective-permute-start.9 = (bf16[192,1536]{1,0:T(8,128)(2,1)S(1)}, bf16[192,1536]{1,0:T(8,128)(2,1)S(1)}, u32[]{:S(2)}, u32[]{:S(2)}) collective-permute-start(bf16[192,1536]{1,0:T(8,128)(2,1)S(1)} %get-tuple-element.195), channel_id=1, source_target_pairs={{0,8},{8,0},{16,24},{24,16},{1,9},{9,1},{17,25},{25,17},{2,10},{10... | collective-permute-start | bytes 1769480 | tf_op jit(solution)/shard_map/ppermute | solution.py:672
  176.2 59.3 %collective-permute-start.17 = (bf16[384,768]{1,0:T(8,128)(2,1)}, bf16[384,768]{1,0:T(8,128)(2,1)}, u32[]{:S(2)}, u32[]{:S(2)}) collective-permute-start(bf16[384,768]{1,0:T(8,128)(2,1)} %get-tuple-element.188), channel_id=1, source_target_pairs={{0,16},{8,24},{16,0},{24,8},{1,17},{9,25},{17,1},{25,9},{2,18},{10... | collective-permute-start | bytes 1769480 | tf_op jit(solution)/shard_map/ppermute | solution.py:672
  180.5 55.0 %collective-permute-start.14 = (bf16[192,1816]{1,0:T(8,128)(2,1)}, bf16[192,1816]{1,0:T(8,128)(2,1)S(1)}, u32[]{:S(2)}, u32[]{:S(2)}) collective-permute-start(bf16[192,1816]{1,0:T(8,128)(2,1)} %get-tuple-element.184), channel_id=1, source_target_pairs={{0,16},{8,24},{16,0},{24,8},{1,17},{9,25},{17,1},{25,9},{2,18},{10... | collective-permute-start | bytes 2092040 | tf_op jit(solution)/shard_map/ppermute | solution.py:672
  182.1 53.4 %collective-permute-start.11 = (bf16[192,1536]{1,0:T(8,128)(2,1)}, bf16[192,1536]{1,0:T(8,128)(2,1)S(1)}, u32[]{:S(2)}, u32[]{:S(2)}) collective-permute-start(bf16[192,1536]{1,0:T(8,128)(2,1)} %get-tuple-element.192), channel_id=1, source_target_pairs={{0,16},{8,24},{16,0},{24,8},{1,17},{9,25},{17,1},{25,9},{2,18},{10... | collective-permute-start | bytes 1769480 | tf_op jit(solution)/shard_map/ppermute | solution.py:672
  183.9 37.3 %collective-permute-start.25 = (f32[96,128]{1,0:T(8,128)S(1)}, f32[96,128]{1,0:T(8,128)S(1)}, u32[]{:S(2)}, u32[]{:S(2)}) collective-permute-start(f32[96,128]{1,0:T(8,128)S(1)} %fusion.12), channel_id=1, source_target_pairs={{0,16},{8,24},{16,0},{24,8},{1,17},{9,25},{17,1},{25,9},{2,18},{10... | collective-permute-start | bytes 147464 | tf_op jit(solution)/shard_map/ppermute | solution.py:672
  229.5 20.9 %collective-permute-start.28 = (f32[96,128]{1,0:T(8,128)S(1)}, f32[96,128]{1,0:T(8,128)S(1)}, u32[]{:S(2)}, u32[]{:S(2)}) collective-permute-start(f32[96,128]{1,0:T(8,128)S(1)} %add.137), channel_id=1, source_target_pairs={{0,4},{1,5},{2,6},{3,7},{4,0},{5,1},{6,2},{7,3},{8,12},{9,13},{10,... | collective-permute-start | bytes 147464 | tf_op jit(solution)/shard_map/ppermute | solution.py:672
  263.6 5.2 %collective-permute-start.21 = (f32[8,4224]{1,0:T(8,128)}, f32[8,4224]{1,0:T(8,128)S(1)}, u32[]{:S(2)}, u32[]{:S(2)}) collective-permute-start(f32[8,4224]{1,0:T(8,128)} %get-tuple-element.81), channel_id=1, source_target_pairs={{0,1},{1,0},{2,3},{3,2},{4,5},{5,4},{6,7},{7,6},{8,9},{9,8},{10,11... | collective-permute-start | bytes 405512 | tf_op jit(solution)/shard_map/ppermute | solution.py:672
  269.7 5.1 %collective-permute-start.22 = (f32[8,4224]{1,0:T(8,128)S(1)}, f32[8,4224]{1,0:T(8,128)S(1)}, u32[]{:S(2)}, u32[]{:S(2)}) collective-permute-start(f32[8,4224]{1,0:T(8,128)S(1)} %add.131), channel_id=1, source_target_pairs={{0,2},{1,3},{2,0},{3,1},{4,6},{5,7},{6,4},{7,5},{8,10},{9,11},{10,... | collective-permute-start | bytes 405512 | tf_op jit(solution)/shard_map/ppermute | solution.py:672
  274.8 7.4 %collective-permute-start.23 = (f32[8,4224]{1,0:T(8,128)S(1)}, f32[8,4224]{1,0:T(8,128)S(1)}, u32[]{:S(2)}, u32[]{:S(2)}) collective-permute-start(f32[8,4224]{1,0:T(8,128)S(1)} %add.132), channel_id=1, source_target_pairs={{0,4},{1,5},{2,6},{3,7},{4,0},{5,1},{6,2},{7,3},{8,12},{9,13},{10,... | collective-permute-start | bytes 405512 | tf_op jit(solution)/shard_map/ppermute | solution.py:672
  (36 other events, 680.7 us)

commit v2 on v1

--- a/solution.py
+++ b/solution.py
@@ -4,6 +4,7 @@
 from jax.experimental import pallas as pl
 from jax.experimental.pallas import tpu as pltpu
 from jax.sharding import PartitionSpec as P
+
 
 HEADS = 24
 HEADDIM = 64
@@ -17,9 +18,11 @@
 MOMENTUM = 0.9
 RATE = 0.01
 LOG2E = 1.4426950408889634
+GATE_ROW = 5
+NORM_ROW = 6
+HEAD_ROW = 7
 F32 = jnp.float32
 BF16 = jnp.bfloat16
-VMEM_LIMIT = 60 * 1024 * 1024
 
 
 def mm(a, b):
@@ -52,6 +55,12 @@
     return mm(exact, high) + mm(exact, middle) + mm(exact, rest)
 
 
+def mm_nt_three(a, b):
+    a_high, a_rest = split2(a)
+    b_high, b_rest = split2(b)
+    return mm_nt(a_high, b_high) + mm_nt(a_high, b_rest) + mm_nt(a_rest, b_high)
+
+
 def mm_three(a, b):
     a_high, a_rest = split2(a)
     b_high, b_rest = split2(b)
@@ -66,6 +75,14 @@
     return jnp.maximum(v, 0.0) + jnp.log1p(jnp.exp(-jnp.abs(v)))
 
 
+def hbm(array):
+    return pltpu.with_memory_space_constraint(array, pltpu.HBM)
+
+
+def vmem(array):
+    return pltpu.with_memory_space_constraint(array, pltpu.VMEM)
+
+
 def whole_spec(array):
     rank = len(array.shape)
     return pl.BlockSpec(array.shape, lambda i, *_: (0,) * rank)
@@ -79,8 +96,12 @@
 SMEM = pl.BlockSpec(memory_space=pltpu.SMEM)
 
 
-def params():
-    return pltpu.CompilerParams(dimension_semantics=("arbitrary",), vmem_limit_bytes=VMEM_LIMIT)
+def params(mib):
+    return pltpu.CompilerParams(dimension_semantics=("arbitrary",), vmem_limit_bytes=mib * 1024 * 1024)
+
+
+def cost(micros):
+    return pl.CostEstimate(flops=int(micros * 1e9), bytes_accessed=int(micros * 3e6), transcendentals=0)
 
 
 def fetch(place, pieces, buffer, sems):
@@ -172,16 +193,15 @@
     length, width = x.shape
     steps = length // Q
     count = len(pieces)
-    cols = pieces[0].shape[1]
     outs = (
-        jax.ShapeDtypeStruct((length, width), BF16),
-        jax.ShapeDtypeStruct((length, CONVDIM), BF16),
-        jax.ShapeDtypeStruct((length, CONVDIM), BF16),
-        jax.ShapeDtypeStruct((length, CONVDIM), BF16),
-        jax.ShapeDtypeStruct((length, INNER), BF16),
-        jax.ShapeDtypeStruct((length, HEADS), F32),
-        jax.ShapeDtypeStruct((length, HEADS), F32),
-        jax.ShapeDtypeStruct((steps, STATE, INNER), BF16),
+        pltpu.HBM((length, width), BF16),
+        pltpu.HBM((length, CONVDIM), BF16),
+        pltpu.HBM((length, CONVDIM), BF16),
+        pltpu.HBM((length, CONVDIM), BF16),
+        pltpu.HBM((length, INNER), BF16),
+        pltpu.HBM((length, HEADS), F32),
+        pltpu.HBM((length, HEADS), F32),
+        pltpu.HBM((steps, STATE, INNER), BF16),
     )
 
     def kernel(*refs):
@@ -219,9 +239,10 @@
             pltpu.VMEM((STATE, INNER), F32),
             pltpu.SemaphoreType.DMA((count,)),
         ],
-        compiler_params=params(),
+        compiler_params=params(28),
+        cost_estimate=cost(24),
         name="forward_scan",
-    )(place, x, aux, segr, gain, conv, head, tri, spread, *pieces)
+    )(place, hbm(x), aux, segr, gain, conv, head, tri, spread, *pieces)
 
 
 def gate_kernel(count, place, normed_ref, y_ref, values_ref, x_ref, cot_ref, skip_ref, gain_ref, *rest):
@@ -291,10 +312,10 @@
             pl.BlockSpec((8, INNER), lambda i: (0, 0)),
         ],
         out_shape=(
-            jax.ShapeDtypeStruct((length, width), BF16),
-            jax.ShapeDtypeStruct((length, INNER), BF16),
-            jax.ShapeDtypeStruct((length, INNER), BF16),
-            jax.ShapeDtypeStruct((length, INNER), BF16),
+            pltpu.HBM((length, width), BF16),
+            pltpu.HBM((length, INNER), BF16),
+            pltpu.HBM((length, INNER), BF16),
+            pltpu.HBM((length, INNER), BF16),
             jax.ShapeDtypeStruct((8, INNER), F32),
         ),
         scratch_shapes=[
@@ -302,9 +323,10 @@
             pltpu.VMEM((count,) + out_pieces[0].shape, BF16),
             pltpu.SemaphoreType.DMA((count,)),
         ],
-        compiler_params=params(),
+        compiler_params=params(40),
+        cost_estimate=cost(18),
         name="gate_both_ways",
-    )(place, normed, y, active, x, cot, skip, gain, *gate_pieces, *out_pieces)
+    )(place, hbm(normed), hbm(y), hbm(active), hbm(x), hbm(cot), skip, gain, *gate_pieces, *out_pieces)
 
 
 def backward_kernel(
@@ -452,21 +474,26 @@
             pl.BlockSpec((8, 128), lambda i: (0, 0)),
         ],
         out_shape=(
-            jax.ShapeDtypeStruct((length, CONVDIM + HEADS), BF16),
+            pltpu.HBM((length, CONVDIM + HEADS), BF16),
             jax.ShapeDtypeStruct((8, CONVDIM), F32),
             jax.ShapeDtypeStruct((8, 128), F32),
         ),
         scratch_shapes=[pltpu.VMEM((Q + 8, CONVDIM), F32), pltpu.VMEM((STATE, INNER), F32)],
-        compiler_params=params(),
+        compiler_params=params(28),
+        cost_estimate=cost(40),
         name="backward_scan",
-    )(dy, active, cin, dsilu, v, cum, states, aux, segr, conv, head, skip, triu, spread, gather)
-
-
-def input_kernel(count, place, dgate_ref, dproj_ref, x_ref, cot_ref, gain_ref, *rest):
+    )(
+        hbm(dy), hbm(active), hbm(cin), hbm(dsilu), hbm(v), hbm(cum), hbm(states), aux, segr, conv, head, skip, triu, spread, gather
+    )
+
+
+def input_kernel(
+    count, place, dgate_ref, dproj_ref, x_ref, cot_ref, gain_ref, conv_sums, head_sums, gate_sums, gather_ref, *rest
+):
     gate_pieces = rest[:count]
     conv_pieces = rest[count : 2 * count]
-    grad_ref, sums_ref = rest[2 * count : 2 * count + 2]
-    gate_w, conv_w, sems = rest[2 * count + 2 :]
+    grad_ref, small_ref = rest[2 * count : 2 * count + 2]
+    gate_w, conv_w, sums_ref, sems = rest[2 * count + 2 :]
     step = pl.program_id(0)
 
     @pl.when(step == 0)
@@ -487,8 +514,20 @@
     grad = inv * (d_normed * gain - unit * jnp.mean(product * gain, axis=-1, keepdims=True))
     grad_ref[...] = cot_ref[...].astype(F32) + grad
 
-
-def input_call(place, dgate, dproj, x, cot, gain, gate_pieces, conv_pieces, rows):
+    @pl.when(step == pl.num_programs(0) - 1)
+    def _():
+        width = gain.shape[1]
+        small_ref[...] = jnp.zeros_like(small_ref)
+        small_ref[0 : CONV + 1, :] = conv_sums[0 : CONV + 1, :]
+        small_ref[GATE_ROW : GATE_ROW + 1, :INNER] = gate_sums[0:1, :]
+        small_ref[NORM_ROW : NORM_ROW + 1, :width] = sums_ref[0:1, :]
+        skip = mm_two(jnp.broadcast_to(gate_sums[1:2, :], (8, INNER)), gather_ref[...])[0:1, :]
+        small_ref[HEAD_ROW : HEAD_ROW + 1, 0:128] = head_sums[0:1, :]
+        small_ref[HEAD_ROW : HEAD_ROW + 1, 128:256] = head_sums[1:2, :]
+        small_ref[HEAD_ROW : HEAD_ROW + 1, 256:384] = skip
+
+
+def input_call(place, dgate, dproj, x, cot, gain, conv_sums, head_sums, gate_sums, gather, gate_pieces, conv_pieces, rows):
     length, width = x.shape
     count = len(gate_pieces)
 
@@ -505,24 +544,45 @@
             row_spec(rows, width),
             row_spec(rows, width),
             whole_spec(gain),
+            whole_spec(conv_sums),
+            whole_spec(head_sums),
+            whole_spec(gate_sums),
+            whole_spec(gather),
         ]
         + [ANY] * (2 * count),
-        out_specs=[row_spec(rows, width), pl.BlockSpec((8, width), lambda i: (0, 0))],
-        out_shape=(jax.ShapeDtypeStruct((length, width), F32), jax.ShapeDtypeStruct((8, width), F32)),
+        out_specs=[row_spec(rows, width), pl.BlockSpec((8, CONVDIM), lambda i: (0, 0))],
+        out_shape=(pltpu.HBM((length, width), F32), jax.ShapeDtypeStruct((8, CONVDIM), F32)),
         scratch_shapes=[
             pltpu.VMEM((count,) + gate_pieces[0].shape, BF16),
             pltpu.VMEM((count,) + conv_pieces[0].shape, BF16),
+            pltpu.VMEM((8, width), F32),
             pltpu.SemaphoreType.DMA((count,)),
         ],
-        compiler_params=params(),
+        compiler_params=params(36),
+        cost_estimate=cost(14),
         name="input_grad",
-    )(place, dgate, dproj, x, cot, gain, *gate_pieces, *conv_pieces)
+    )(place, hbm(dgate), hbm(dproj), hbm(x), hbm(cot), gain, conv_sums, head_sums, gate_sums, gather, *gate_pieces, *conv_pieces)
+
+
+def up(value, unit):
+    return -(-value // unit) * unit
 
 
 def left_kernel(
-    gate_a, gate_b, conv_a, conv_b, out_a, out_b, err_in, err_out, start_in, start_out,
-    grad_in, grad_out, whole_in, whole_out, left_ref
+    gate_a, gate_b, conv_a, conv_b, out_a, out_b, err_in, err_out, start_in, start_out, small_ref,
+    grad_in, grad_out, whole_in, whole_out, left_ref, tall
 ):
+    step = pl.program_id(0)
+    rows_in = err_in.shape[0]
+    rows_out = err_out.shape[0]
+    begin = rows_in * pl.num_programs(0)
+    rank = start_in.shape[0]
+    lead = tall.shape[0]
+
+    @pl.when(step == 0)
+    def _():
+        tall[...] = jnp.zeros_like(tall)
+
     gate = gate_a[...].astype(F32) + gate_b[...].astype(F32)
     conv = conv_a[...].astype(F32) + conv_b[...].astype(F32)
     out = out_a[...].astype(F32) + out_b[...].astype(F32)
@@ -535,38 +595,49 @@
     whole_in[:, :INNER] = gate
     whole_in[:, INNER:] = conv
     whole_out[...] = out
-    left_in = mm_three(gate, start_in[:INNER, :]) + mm_three(conv, start_in[INNER:, :])
-    left_out = mm_three(out, start_out[...])
-    tall = jnp.concatenate([left_in, left_out], axis=0)
-    rank = tall.shape[1]
-    tall = jnp.concatenate([tall, jnp.zeros((tall.shape[0], 128 - rank), F32)], axis=1)
-    extra = left_ref.shape[1] - tall.shape[0]
-    if extra:
-        tall = jnp.concatenate([tall, jnp.zeros((extra, 128), F32)], axis=0)
-    left_ref[...] = tall.T[:rank, :]
-
-
-def up(value, unit):
-    return -(-value // unit) * unit
-
-
-def left_call(gate, conv, out, err_in, err_out, start_in, start_out):
+    left_in = mm_nt_three(gate, start_in[:, :INNER]) + mm_nt_three(conv, start_in[:, INNER:])
+    tall[pl.ds(pl.multiple_of(step * rows_in, 8), rows_in), :rank] = left_in
+    tall[pl.ds(pl.multiple_of(begin + step * rows_out, 8), rows_out), :rank] = mm_nt_three(out, start_out[...])
+
+    @pl.when(step == pl.num_programs(0) - 1)
+    def _():
+        left_ref[:, :lead] = tall[...].T[:rank, :]
+        left_ref[:, lead:] = small_ref[...]
+
+
+def left_call(gate, conv, out, err_in, err_out, start_in, start_out, small, blocks):
     rows_in, cols_in = err_in.shape
     rows_out, cols_out = err_out.shape
-    rank = start_in.shape[1]
-    shapes = (
-        jax.ShapeDtypeStruct((rows_in, cols_in), F32),
-        jax.ShapeDtypeStruct((rows_out, cols_out), F32),
-        jax.ShapeDtypeStruct((rows_in, cols_in), F32),
-        jax.ShapeDtypeStruct((rows_out, cols_out), F32),
-        jax.ShapeDtypeStruct((rank, up(rows_in + rows_out, 128)), F32),
-    )
+    rank = start_in.shape[0]
+    lead = up(rows_in + rows_out, 128)
+    assert rank == small.shape[0]
+    part_in, part_out = rows_in // blocks, rows_out // blocks
+
+    def both(rows_a, cols_a, rows_b, cols_b):
+        return [row_spec(rows_a, cols_a), row_spec(rows_b, cols_b)]
+
+    width = lead + small.shape[1]
     return pl.pallas_call(
         left_kernel,
-        out_shape=shapes,
-        compiler_params=pltpu.CompilerParams(vmem_limit_bytes=VMEM_LIMIT),
+        grid=(blocks,),
+        in_specs=[row_spec(part_in, INNER)] * 2
+        + [row_spec(part_in, cols_in - INNER)] * 2
+        + [row_spec(part_out, cols_out)] * 2
+        + both(part_in, cols_in, part_out, cols_out)
+        + [whole_spec(start_in), whole_spec(start_out), whole_spec(small)],
+        out_specs=both(part_in, cols_in, part_out, cols_out) * 2 + [pl.BlockSpec((rank, width), lambda i: (0, 0))],
+        out_shape=[
+            pltpu.HBM((rows_in, cols_in), F32),
+            pltpu.HBM((rows_out, cols_out), F32),
+            pltpu.VMEM((rows_in, cols_in), F32),
+            pltpu.VMEM((rows_out, cols_out), F32),
+        ]
+        + [jax.ShapeDtypeStruct((rank, width), F32)],
+        scratch_shapes=[pltpu.VMEM((lead, 128), F32)],
+        compiler_params=params(24),
+        cost_estimate=cost(6),
         name="left_factors",
-    )(*gate, *conv, *out, err_in, err_out, start_in, start_out)
+    )(*gate, *conv, *out, hbm(err_in), hbm(err_out), start_in, start_out, small)
 
 
 def gram_schmidt(rows):
@@ -580,68 +651,82 @@
     return rows
 
 
-def right_kernel(left_ref, whole_in, whole_out, hat_in, hat_out, right_ref):
+def right_kernel(lead, left_a, left_b, whole_in, whole_out, hat_in, hat_out, tall_in, tall_out, right_ref, small_ref):
     rows_in, cols_in = whole_in.shape
     rows_out, cols_out = whole_out.shape
-    rank = left_ref.shape[0]
-    left = left_ref[...]
+    rank = left_a.shape[0]
+    left = left_a[:, :lead] + left_b[:, :lead]
+    small_ref[...] = left_a[:, lead:] + left_b[:, lead:]
     places = lax.broadcasted_iota(jnp.int32, left.shape, 1)
     both_in = gram_schmidt(jnp.where(places < rows_in, left, 0.0))
     both_out = gram_schmidt(jnp.where((places >= rows_in) & (places < rows_in + rows_out), left, 0.0))
-    tall = jnp.concatenate([both_in + both_out, jnp.zeros((128 - rank, left.shape[1]), F32)], axis=0).T
-    hat_in[...] = tall[:rows_in, :rank]
-    hat_out[...] = tall[rows_in : rows_in + rows_out, :rank]
+    hats = both_in + both_out
+    hat_in[...] = hats[:, :rows_in]
+    hat_out[...] = hats[:, rows_in : rows_in + rows_out]
+    tall = jnp.concatenate([hats, jnp.zeros((128 - rank, lead), F32)], axis=0).T
+    tall_in[...] = tall[:rows_in, :rank]
+    tall_out[...] = tall[rows_in : rows_in + rows_out, :rank]
     right_ref[:, :cols_in] = mm_three(both_in[:, :rows_in], whole_in[...])
     out_rows = both_out[:, rows_in : rows_in + rows_out]
     right_ref[:, up(cols_in, 128) : up(cols_in, 128) + cols_out] = mm_three(out_rows, whole_out[...])
 
 
-def right_call(left, whole_in, whole_out):
-    rank = left.shape[0]
+def right_call(lead, left, whole_in, whole_out):
+    rank, total = left[0].shape
     width = up(whole_in.shape[1], 128) + up(whole_out.shape[1], 128)
+    rows_in, rows_out = whole_in.shape[0], whole_out.shape[0]
+
+    def kernel(*refs):
+        right_kernel(lead, *refs)
+
     return pl.pallas_call(
-        right_kernel,
+        kernel,
         out_shape=(
-            jax.ShapeDtypeStruct((whole_in.shape[0], rank), F32),
-            jax.ShapeDtypeStruct((whole_out.shape[0], rank), F32),
+            jax.ShapeDtypeStruct((rank, rows_in), F32),
+            jax.ShapeDtypeStruct((rank, rows_out), F32),
+            jax.ShapeDtypeStruct((rows_in, rank), F32),
+            jax.ShapeDtypeStruct((rows_out, rank), F32),
             jax.ShapeDtypeStruct((rank, width), F32),
+            jax.ShapeDtypeStruct((rank, total - lead), F32),
         ),
-        compiler_params=pltpu.CompilerParams(vmem_limit_bytes=VMEM_LIMIT),
+        compiler_params=pltpu.CompilerParams(vmem_limit_bytes=24 * 1024 * 1024),
+        cost_estimate=cost(5),
         name="right_factors",
-    )(left, whole_in, whole_out)
+    )(*left, vmem(whole_in), vmem(whole_out))
 
 
 def final_kernel(
-    scale, right_ref, hat_in, whole_in, mom_in, mas_in, hat_out, whole_out, mom_out, mas_out,
-    right_in_ref, err_in, new_mom_in, new_mas_in, right_out_ref, err_out, new_mom_out, new_mas_out
+    scale, right_a, right_b, hat_in, whole_in, mom_in, mas_in, hat_out, whole_out, mom_out, mas_out,
+    right_in_ref, err_in, new_mom_in, new_mas_in, right_out_ref, err_out, new_mom_out, new_mas_out, three
 ):
     cols_in = whole_in.shape[1]
     cols_out = whole_out.shape[1]
     skip = up(cols_in, 128)
-    rank = right_ref.shape[0]
 
     @pl.when(pl.program_id(0) == 0)
     def _():
-        right = right_ref[...] * scale
-        tall = jnp.concatenate([right, jnp.zeros((128 - rank, right.shape[1]), F32)], axis=0).T
-        right_in_ref[...] = tall[:cols_in, :rank]
-        right_out_ref[...] = tall[skip : skip + cols_out, :rank]
-
-    def one(hat, right, whole, mom, mas, err, new_mom, new_mas):
-        approx = mm_three(hat[...], right)
+        right = (right_a[...] + right_b[...]) * scale
+        right_in_ref[...] = right[:, :cols_in]
+        right_out_ref[...] = right[:, skip : skip + cols_out]
+        high = right.astype(BF16).astype(F32)
+        three[...] = jnp.concatenate([high, right - high, high], axis=0).astype(BF16)
+
+    def one(hat_ref, begin, whole, mom, mas, err, new_mom, new_mas):
+        hat = hat_ref[...]
+        high = hat.astype(BF16).astype(F32)
+        left = jnp.concatenate([high, high, hat - high], axis=1).astype(BF16)
+        approx = mm(left, three[:, begin : begin + whole.shape[1]])
         err[...] = whole[...] - approx
-        fresh = MOMENTUM * mom[...] + approx
+        fresh = mom[...] + approx
         new_mom[...] = fresh
         new_mas[...] = mas[...] - RATE * fresh
 
-    one(hat_in, right_ref[:, :cols_in] * scale, whole_in, mom_in, mas_in, err_in, new_mom_in, new_mas_in)
-    one(
-        hat_out, right_ref[:, skip : skip + cols_out] * scale, whole_out, mom_out, mas_out, err_out, new_mom_out, new_mas_out
-    )
+    one(hat_in, 0, whole_in, mom_in, mas_in, err_in, new_mom_in, new_mas_in)
+    one(hat_out, skip, whole_out, mom_out, mas_out, err_out, new_mom_out, new_mas_out)
 
 
 def final_call(scale, right, hat_in, whole_in, mom_in, mas_in, hat_out, whole_out, mom_out, mas_out, blocks):
-    rank = right.shape[0]
+    rank, width = right[0].shape
 
     def kernel(*refs):
         final_kernel(scale, *refs)
@@ -650,21 +735,80 @@
         return [row_spec(rows // blocks, rank)] + [row_spec(rows // blocks, cols)] * 3
 
     def out_specs(rows, cols):
-        return [pl.BlockSpec((cols, rank), lambda i: (0, 0))] + [row_spec(rows // blocks, cols)] * 3
+        return [pl.BlockSpec((rank, cols), lambda i: (0, 0))] + [row_spec(rows // blocks, cols)] * 3
 
     def shapes(rows, cols):
-        return [jax.ShapeDtypeStruct((cols, rank), F32)] + [jax.ShapeDtypeStruct((rows, cols), F32)] * 3
+        return [jax.ShapeDtypeStruct((rank, cols), F32)] + [pltpu.HBM((rows, cols), F32)] * 3
 
     size_in, size_out = whole_in.shape, whole_out.shape
     return pl.pallas_call(
         kernel,
         grid=(blocks,),
-        in_specs=[whole_spec(right)] + specs(*size_in) + specs(*size_out),
+        in_specs=[whole_spec(right[0])] * 2 + specs(*size_in) + specs(*size_out),
         out_specs=out_specs(*size_in) + out_specs(*size_out),
         out_shape=shapes(*size_in) + shapes(*size_out),
-        compiler_params=params(),
+        scratch_shapes=[pltpu.VMEM((3 * rank, width), BF16)],
+        compiler_params=params(24),
+        cost_estimate=cost(10),
         name="final_update",
-    )(right, hat_in, whole_in, mom_in, mas_in, hat_out, whole_out, mom_out, mas_out)
+    )(
+        *right, hat_in, vmem(whole_in), vmem(mom_in), vmem(mas_in), hat_out, vmem(whole_out), vmem(mom_out), vmem(mas_out)
+    )
+
+
+def decay_call(arrays, blocks):
+    count = len(arrays)
+    specs = [row_spec(array.shape[0] // blocks, array.shape[1]) for array in arrays]
+
+    def kernel(*refs):
+        for index in range(count):
+            value = refs[index][...]
+            refs[count + index][...] = MOMENTUM * value if index % 2 == 0 else value
+
+    return pl.pallas_call(
+        kernel,
+        grid=(blocks,),
+        in_specs=specs,
+        out_specs=specs,
+        out_shape=[pltpu.VMEM(array.shape, F32) for array in arrays],
+        compiler_params=params(12),
+        cost_estimate=cost(3),
+        name="states_to_vmem",
+    )(*[hbm(array) for array in arrays])
+
+
+def small_kernel(replicas, sums_a, sums_b, conv_mom, conv_mas, head_mom, head_mas, norm_mom, norm_mas, gate_mom, gate_mas, *outs):
+    width = norm_mom.shape[1]
+    sums = sums_a[...] + sums_b[...]
+    head = [sums[HEAD_ROW : HEAD_ROW + 1, 128 * k : 128 * k + HEADS] for k in range(3)]
+    grads = (
+        sums[0 : CONV + 1, :],
+        jnp.concatenate(head, axis=0),
+        sums[NORM_ROW : NORM_ROW + 1, :width],
+        sums[GATE_ROW : GATE_ROW + 1, :INNER],
+    )
+    pairs = ((conv_mom, conv_mas), (head_mom, head_mas), (norm_mom, norm_mas), (gate_mom, gate_mas))
+    for index, (grad, (moment, master)) in enumerate(zip(grads, pairs)):
+        fresh = MOMENTUM * moment[...] + grad / replicas
+        for place, value in enumerate((grad, fresh, master[...] - RATE * fresh)):
+            out = outs[3 * index + place]
+            out[...] = value.reshape(out.shape)
+
+
+def small_call(replicas, sums_a, sums_b, *states):
+    def kernel(*refs):
+        small_kernel(replicas, *refs)
+
+    shapes = []
+    for state in states[::2]:
+        shapes += [jax.ShapeDtypeStruct(state.shape[1:] if state.shape[0] == 1 else state.shape, F32)] * 3
+    return pl.pallas_call(
+        kernel,
+        out_shape=shapes,
+        compiler_params=pltpu.CompilerParams(vmem_limit_bytes=8 * 1024 * 1024),
+        cost_estimate=cost(2),
+        name="small_update",
+    )(sums_a, sums_b, *states)
 
 
 def flip(value, axis, bit):
@@ -686,36 +830,41 @@
     return [pieces[index] for index in range(len(pieces))]
 
 
-def scatter_pieces(whole, axis):
+def slice_pieces(whole, axis):
     size = lax.axis_size(axis)
     place = lax.axis_index(axis)
     rows = whole.shape[0] // size
-    pieces = {
+    return {
         index: lax.dynamic_slice_in_dim(whole, jnp.bitwise_xor(place, index) * rows, rows, 0) for index in range(size)
     }
+
+
+def halve(pieces, axis, bit):
+    arrived = {index: flip(pieces[index | bit], axis, bit) for index in sorted(pieces) if not index & bit}
+    return {index: (pieces[index].astype(F32) + arrived[index].astype(F32)).astype(BF16) for index in arrived}
+
+
+def halve_first(whole, axis):
+    pieces = slice_pieces(whole, axis)
+    for bit in bits_of(axis)[:-1]:
+        pieces = halve(pieces, axis, bit)
+    return pieces
+
+
+def halve_last(pieces, axis):
+    bit = bits_of(axis)[-1]
+    return pieces[0], flip(pieces[bit], axis, bit)
+
+
+def sum_pair(value, axis):
     bits = bits_of(axis)
-    for bit in bits:
-        arrived = {index: flip(pieces[index | bit], axis, bit) for index in sorted(pieces) if not index & bit}
-        if bit == bits[-1]:
-            return pieces[0], arrived[0]
-        pieces = {
-            index: (pieces[index].astype(F32) + arrived[index].astype(F32)).astype(BF16) for index in arrived
-        }
-
-
-def sum_all(value, axis):
-    for bit in bits_of(axis):
+    for bit in bits[:-1]:
         value = value + flip(value, axis, bit)
-    return value
+    return value, flip(value, axis, bits[-1])
 
 
 def rows_product(left, right):
     return lax.dot_general(left, right, (((0,), (0,)), ((), ())), preferred_element_type=F32).astype(BF16)
-
-
-def plain_update(grad_sum, moment, master, replicas):
-    moment_new = MOMENTUM * moment + grad_sum / replicas
-    return (moment_new, master - RATE * moment_new)
 
 
 def position_table(ids):
@@ -736,7 +885,7 @@
     return jnp.stack(columns, axis=1)
 
 
-def on_device(
+def layer_step(
     tokens,
     segment_ids,
     cotangent,
@@ -760,7 +909,7 @@
     replicas = lax.axis_size("rep")
     x = tokens[0]
     cot = cotangent[0]
-    length, width = x.shape
+    length, _ = x.shape
     place = lax.axis_index("grp").astype(jnp.int32).reshape(1)
     conv_w = gather_pieces(in_proj_master[:, INNER:].astype(BF16), "grp")
     gate_w = gather_pieces(in_proj_master[:, :INNER].astype(BF16), "grp")
@@ -784,61 +933,47 @@
     output, mixed, d_gate, d_result, gate_sums = gate_call(
         place, normed, y, active, x, cot, skip, gate_gain[None], gate_w, out_w, 256
     )
-    out_pair = scatter_pieces(rows_product(mixed, cot), "grp")
-    gate_pair = scatter_pieces(rows_product(normed, d_gate), "grp")
+    gate_pieces = halve_first(rows_product(normed, d_gate), "grp")
+    out_pieces = halve_first(rows_product(mixed, cot), "grp")
+    gate_pair = halve_last(gate_pieces, "grp")
+    out_pair = halve_last(out_pieces, "grp")
     d_proj, conv_sums, head_sums = backward_call(
         d_result, active, cin, dsilu, v, cum, states, aux, segr, conv, head, skip, triu, spread, gather
     )
-    conv_pair = scatter_pieces(rows_product(normed, d_proj), "grp")
-    input_grad, norm_sums = input_call(place, d_gate, d_proj, x, cot, norm_gain[None], gate_w, conv_w, 256)
-
-    skip_grad = jnp.sum(gate_sums[1].reshape(HEADS, HEADDIM), axis=1)
-    small = jnp.concatenate(
-        [
-            conv_sums[: CONV + 1].reshape(-1),
-            head_sums[0, :HEADS],
-            head_sums[1, :HEADS],
-            skip_grad,
-            norm_sums[0],
-            gate_sums[0],
-        ]
-    )
-    count = small.shape[0]
-    small = jnp.pad(small, (0, up(count, 1024) - count)).reshape(-1, 128)
-    small = sum_all(sum_all(small, "grp"), "rep").reshape(-1)
-    sizes = [(CONV + 1) * CONVDIM, 3 * HEADS, width, INNER]
-    parts = []
-    begin = 0
-    for size in sizes:
-        parts.append(small[begin : begin + size])
-        begin += size
-    conv_grad = parts[0].reshape(CONV + 1, CONVDIM)
-    head_grad = parts[1].reshape(3, HEADS)
-    norm_gain_grad, gate_gain_grad = parts[2], parts[3]
-
+    conv_pair = halve_last(halve_first(rows_product(normed, d_proj), "grp"), "grp")
+    input_grad, small = input_call(
+        place, d_gate, d_proj, x, cot, norm_gain[None], conv_sums, head_sums, gate_sums, gather, gate_w, conv_w, 512
+    )
     in_shard, out_shard, whole_in, whole_out, left = left_call(
-        gate_pair, conv_pair, out_pair, in_proj_error[0], out_proj_error[0], in_proj_start[0], out_proj_start[0]
-    )
-    left = sum_all(left, "rep")
-    hat_in, hat_out, right = right_call(left, whole_in, whole_out)
-    right = sum_all(right, "rep")
+        gate_pair, conv_pair, out_pair, in_proj_error[0], out_proj_error[0], in_proj_start[0].T, out_proj_start[0].T, small, 4
+    )
+    lead = left.shape[1] - small.shape[1]
+    left = sum_pair(left, "rep")
+    hat_in, hat_out, tall_in, tall_out, right, small = right_call(lead, left, whole_in, whole_out)
+    mom_in, mas_in, mom_out, mas_out = decay_call(
+        (in_proj_moment, in_proj_master, out_proj_moment, out_proj_master), 4
+    )
+    right = sum_pair(right, "rep")
+    small = sum_pair(small, "grp")
+    (
+        conv_grad, conv_mom, conv_new, head_grad, head_mom, head_new,
+        norm_gain_grad, gain_mom, gain_new, gate_gain_grad, gate_mom, gate_new,
+    ) = small_call(
+        replicas, *small, conv_moment, conv_master, head_moment, head_master,
+        norm_gain_moment[None], norm_gain[None], gate_gain_moment[None], gate_gain[None],
+    )
     right_in, in_err, in_mom, in_new, right_out, out_err, out_mom, out_new = final_call(
-        1.0 / replicas, right, hat_in, whole_in, in_proj_moment, in_proj_master,
-        hat_out, whole_out, out_proj_moment, out_proj_master, 4,
-    )
-    conv_mom, conv_new = plain_update(conv_grad, conv_moment, conv_master, replicas)
-    head_mom, head_new = plain_update(head_grad, head_moment, head_master, replicas)
-    gain_mom, gain_new = plain_update(norm_gain_grad, norm_gain_moment, norm_gain, replicas)
-    gate_mom, gate_new = plain_update(gate_gain_grad, gate_gain_moment, gate_gain, replicas)
+        1.0 / replicas, right, tall_in, whole_in, mom_in, mas_in, tall_out, whole_out, mom_out, mas_out, 4
+    )
     return (
         output[None],
         input_grad[None],
         in_shard[None],
         out_shard[None],
-        hat_in,
-        hat_out,
-        right_in[None],
-        right_out[None],
+        hat_in.T,
+        hat_out.T,
+        right_in.T[None],
+        right_out.T[None],
         in_err[None],
         out_err[None],
         in_mom,
@@ -862,7 +997,7 @@
 
 def solution(mesh):
     return jax.shard_map(
-        on_device,
+        layer_step,
         mesh=mesh,
         in_specs=(
             P(("grp", "rep"), None, None),

time: 299 us -> 237 us (0.79)
  local copies, waits for them, and re-layouts: 25.6 us -> 2.38 us
  waiting for transfers between devices: 96.2 us -> 76.2 us
  other arithmetic: 18.9 us -> 3.7 us
  Pallas kernels: 120 us -> 113 us
    ppermute x29 -> x26, waiting for transfers between devices: 96.2 us -> 76.2 us  [flip(): return lax.ppermute(value, axis, [(i, i ^ bit) for i in range(size)])]
    unnamed x70 -> x32, local copies, waits for them, and re-layouts: 15.7 us -> 0.99 us
    convert_element_type x8, other arithmetic: 10.3 us -> 1.39 us  [the longest x3 1.02 us: halve(): (pieces[index].astype(F32) + arrived[index].astype(F32)).astype(BF16)]
    pallas_call x3 -> x5, Pallas kernels: 24.1 us -> 17.7 us  [the longest x1 5.59 us: left_call(): pl.pallas_call(left_kernel, grid=(blocks,), in_specs=[row_spec(part_in, I...]
    ppermute x29 -> x26, starting transfers between devices: 24.1 us -> 26.6 us  [flip(): return lax.ppermute(value, axis, [(i, i ^ bit) for i in range(size)])]
  transfers between devices with their start and end apart: 29 -> 26, of which waited for: 12 -> 11; matrix products, arithmetic and copies ran while one was open for 12% -> 5% of each run, Pallas kernels for 15% -> 35%
where the time goes in v2:
time: 237 us
  Pallas kernels  113 us (48%)
  waiting for transfers between devices  76.2 us (32%)
  starting transfers between devices  26.6 us (11%)
  matrix products  13.5 us (6%)
  other arithmetic  3.7 us (2%)
  local copies, waits for them, and re-layouts  2.38 us (1%)
    ppermute x26, waiting for transfers between devices, flip(): return lax.ppermute(value, axis, [(i, i ^ bit) for i in range(size)])  76.2 us
    pallas_call x1, Pallas kernels, backward_call(): pl.pallas_call(backward_kernel, grid=(steps,), in_specs=[row_spec(Q, INNE...  39.7 us
    ppermute x26, starting transfers between devices, flip(): return lax.ppermute(value, axis, [(i, i ^ bit) for i in range(size)])  26.6 us
    pallas_call x1, Pallas kernels, forward_call(): pl.pallas_call(kernel, grid=(steps,), in_specs=[SMEM, row_spec(Q, width),...  23.7 us
    pallas_call x1, Pallas kernels, gate_call(): pl.pallas_call(kernel, grid=(length // rows,), in_specs=[SMEM, row_spec(r...  17.4 us
    pallas_call x1, Pallas kernels, input_call(): pl.pallas_call(kernel, grid=(length // rows,), in_specs=[SMEM, row_spec(r...  14.6 us
    dot_general x3, matrix products, rows_product(): lax.dot_general(left, right, (((0,), (0,)), ((), ())), preferred_element_...  13.5 us
    pallas_call x1, Pallas kernels, left_call(): pl.pallas_call(left_kernel, grid=(blocks,), in_specs=[row_spec(part_in, I...  5.59 us
  transfers between devices with their start and end apart: 26, of which 11 were waited for; matrix products, arithmetic and copies ran while one was open for 5% of the time, Pallas kernels for 35%

profile of v2, /device:TPU:0, one launch (start us, length us, event | category | flops | bytes accessed | tf_op | source)
XLA Modules:
  0.0 236.8 jit_solution(5697598920700338522)
XLA Ops:
  0.7 2.0 convert.8
  2.8 3.1 %collective-permute-start.1 = (bf16[192,1816]{1,0:T(8,128)(2,1)S(1)}, bf16[192,1816]{1,0:T(8,128)(2,1)S(1)}, u32[]{:S(2)}, u32[]{:S(2)}) collective-permute-start(bf16[192,1816]{1,0:T(8,128)(2,1)S(1)} %slice.69.refs_9_.refs_14_), channel_id=1, source_target_pairs={{0,16},{8,24},{16,0},{24,8},{1,17},{9,25},{17,1},{25,9},{2,18},{10... | collective-permute-start | bytes 2092040 | tf_op jit(solution)/shard_map/ppermute | solution.py:816
  9.3 13.8 %collective-permute-done.1.refs_11_.refs_16_ = bf16[192,1816]{1,0:T(8,128)(2,1)S(1)} collective-permute-done((bf16[192,1816]{1,0:T(8,128)(2,1)S(1)}, bf16[192,1816]{1,0:T(8,128)(2,1)S(1)}, u32[]{:S(2)}, u32[]{:S(2)}) %collective-permute-start.1) | collective-permute-done | bytes 697376 | tf_op jit(solution)/shard_map/ppermute | solution.py:816
  24.1 11.8 %collective-permute-done.4.refs_10_.refs_12_ = bf16[192,1536]{1,0:T(8,128)(2,1)} collective-permute-done((bf16[192,1536]{1,0:T(8,128)(2,1)S(1)}, bf16[192,1536]{1,0:T(8,128)(2,1)}, u32[]{:S(2)}, u32[]{:S(2)}) %collective-permute-start.4) | collective-permute-done | bytes 589856 | tf_op jit(solution)/shard_map/ppermute | solution.py:816
  35.9 11.8 %collective-permute-done.7.refs_14_ = bf16[384,768]{1,0:T(8,128)(2,1)} collective-permute-done((bf16[384,768]{1,0:T(8,128)(2,1)S(1)}, bf16[384,768]{1,0:T(8,128)(2,1)}, u32[]{:S(2)}, u32[]{:S(2)}) %collective-permute-start.7) | collective-permute-done | bytes 589856 | tf_op jit(solution)/shard_map/ppermute | solution.py:816
  48.2 23.7 %forward_scan.1 = (bf16[1024,768]{1,0:T(8,128)(2,1)}, bf16[1024,1792]{1,0:T(8,128)(2,1)}, bf16[1024,1792]{1,0:T(8,128)(2,1)}, bf16[1024,1792]{1,0:T(8,128)(2,1)}...) custom-call(s32[1]{0:T(128)} %bitcast.refs_0_, ...), custom_call_target="tpu_custom_call" | custom-call | flops 24000000000 | bytes 72000000 | tf_op jit(solution)/shard_map/forward_scan/pallas_call | solution.py:210
  72.0 17.4 %gate_both_ways.1 = (bf16[1024,768]{1,0:T(8,128)(2,1)}, bf16[1024,1536]{1,0:T(8,128)(2,1)}, bf16[1024,1536]{1,0:T(8,128)(2,1)}, bf16[1024,1536]{1,0:T(8,128)(2,1)}, f32[8,1536]{1,0:T(8,128)S(1)}) custom-call(s32[1]{0:T(128)} %bitcast.refs_0_, bf16[1024,768]{1,0:T(8,128)(2,1)} %get-tuple-element.79.refs_1_, bf16[1024,1536]{1,0:T(8,128)(2,1)} %get-tuple-element.80.refs_2_, ...), custom_call_target="tpu_custom_call" | custom-call | flops 17999998976 | bytes 54000000 | tf_op jit(solution)/shard_map/gate_both_ways/pallas_call | solution.py:293
  89.4 4.7 %convolution_convert_fusion = bf16[1536,768]{1,0:T(8,128)(2,1)S(1)} fusion(bf16[1024,1536]{1,0:T(8,128)(2,1)} %get-tuple-element.95, bf16[1,1024,768]{2,1,0:T(8,128)(2,1)S(1)} %copy-done.12), kind=kOutput, calls=%fused_computation | convolution fusion | flops 2417098752 | bytes 7077888 | tf_op jit(solution)/shard_map/dot_general | solution.py:867
  95.6 2.9 %convolution_convert_fusion.1 = bf16[768,1536]{1,0:T(8,128)(2,1)S(1)} fusion(bf16[1024,768]{1,0:T(8,128)(2,1)S(1)} %copy-done.14, bf16[1024,1536]{1,0:T(8,128)(2,1)S(1)} %copy-done.13), kind=kOutput, calls=%fused_computation.1 | convolution fusion | flops 2417098752 | bytes 7077888 | tf_op jit(solution)/shard_map/dot_general | solution.py:867
  99.2 39.7 %backward_scan.1 = (bf16[1024,1816]{1,0:T(8,128)(2,1)}, f32[8,1792]{1,0:T(8,128)S(1)}, f32[8,128]{1,0:T(8,128)S(1)}) custom-call(bf16[1024,1536]{1,0:T(8,128)(2,1)} %get-tuple-element.84.dy_ref, bf16[1024,1792]{1,0:T(8,128)(2,1)} %get-tuple-element.81.refs_3_.active_ref, bf16[1024,1792]{1,0:T(8,128)(2,1)} %get-tuple-element.85.cin_ref, ...), custom_call_target="tpu_custom_call" | custom-call | flops 40000000000 | bytes 120000000 | tf_op jit(solution)/shard_map/backward_scan/pallas_call | solution.py:451
  138.9 5.8 %convolution_convert_fusion.2 = bf16[768,1816]{1,0:T(8,128)(2,1)S(1)} fusion(bf16[1024,768]{1,0:T(8,128)(2,1)S(1)} %copy-done.14, bf16[1024,1816]{1,0:T(8,128)(2,1)} %get-tuple-element.90.refs_2_), kind=kOutput, calls=%fused_computation.2 | convolution fusion | flops 2857715712 | bytes 8081408 | tf_op jit(solution)/shard_map/dot_general | solution.py:867
  150.5 14.6 %input_grad.1 = (f32[1024,768]{1,0:T(8,128)}, f32[8,1792]{1,0:T(8,128)S(1)}) custom-call(s32[1]{0:T(128)} %bitcast.refs_0_, bf16[1024,1536]{1,0:T(8,128)(2,1)} %get-tuple-element.83.refs_1_, bf16[1024,1816]{1,0:T(8,128)(2,1)} %get-tuple-element.90.refs_2_, bf16[1024,768]{1,0:T(8,128)(2,1)} %bitcast.80, bf16[1024,768]{1,0:T(8,128)(2,1)} %bitcast.82, ...), custom_call_target="tpu_custom_call" | custom-call | flops 14000000000 | bytes 42000000 | tf_op jit(solution)/shard_map/input_grad/pallas_call | solution.py:537
  165.1 9.6 %collective-permute-done.11.gate_b = bf16[192,1536]{1,0:T(8,128)(2,1)S(1)} collective-permute-done((bf16[192,1536]{1,0:T(8,128)(2,1)S(1)}, bf16[192,1536]{1,0:T(8,128)(2,1)S(1)}, u32[]{:S(2)}, u32[]{:S(2)}) %collective-permute-start.11) | collective-permute-done | bytes 589856 | tf_op jit(solution)/shard_map/ppermute | solution.py:816
  174.7 15.0 %collective-permute-done.14.conv_b = bf16[192,1816]{1,0:T(8,128)(2,1)S(1)} collective-permute-done((bf16[192,1816]{1,0:T(8,128)(2,1)S(1)}, bf16[192,1816]{1,0:T(8,128)(2,1)S(1)}, u32[]{:S(2)}, u32[]{:S(2)}) %collective-permute-start.14) | collective-permute-done | bytes 697376 | tf_op jit(solution)/shard_map/ppermute | solution.py:816
  189.7 5.6 %left_factors.1 = (f32[192,3352]{1,0:T(8,128)}, f32[384,768]{1,0:T(8,128)}, f32[192,3352]{1,0:T(8,128)S(1)}, f32[384,768]{1,0:T(8,128)S(1)}, f32[8,2432]{1,0:T(8,128)S(1)}) custom-call(bf16[192,1536]{1,0:T(8,128)(2,1)S(1)} %get-tuple-element.141.gate_a, bf16[192,1536]{1,0:T(8,128)(2,1)S(1)} %collective-permute-done.11.gate_b, ...), custom_call_target="tpu_custom_call" | custom-call | flops 6000000000 | bytes 18000000 | tf_op jit(solution)/shard_map/left_factors/pallas_call | solution.py:620
  197.0 2.7 %collective-permute-done.18 = f32[8,2432]{1,0:T(8,128)S(1)} collective-permute-done((f32[8,2432]{1,0:T(8,128)S(1)}, f32[8,2432]{1,0:T(8,128)S(1)}, u32[]{:S(2)}, u32[]{:S(2)}) %collective-permute-start.18) | collective-permute-done | bytes 77856 | tf_op jit(solution)/shard_map/ppermute | solution.py:816
  201.6 2.6 %collective-permute-done.19 = f32[8,2432]{1,0:T(8,128)S(1)} collective-permute-done((f32[8,2432]{1,0:T(8,128)S(1)}, f32[8,2432]{1,0:T(8,128)S(1)}, u32[]{:S(2)}, u32[]{:S(2)}) %collective-permute-start.19) | collective-permute-done | bytes 77856 | tf_op jit(solution)/shard_map/ppermute | solution.py:816
  204.2 3.3 %collective-permute-start.20 = (f32[8,2432]{1,0:T(8,128)S(1)}, f32[8,2432]{1,0:T(8,128)S(1)}, u32[]{:S(2)}, u32[]{:S(2)}) collective-permute-start(f32[8,2432]{1,0:T(8,128)S(1)} %add.97.refs_0_), channel_id=1, source_target_pairs={{0,4},{1,5},{2,6},{3,7},{4,0},{5,1},{6,2},{7,3},{8,12},{9,13},{10,... | collective-permute-start | bytes 233480 | tf_op jit(solution)/shard_map/ppermute | solution.py:816
  207.5 2.4 %collective-permute-done.20.refs_1_ = f32[8,2432]{1,0:T(8,128)S(1)} collective-permute-done((f32[8,2432]{1,0:T(8,128)S(1)}, f32[8,2432]{1,0:T(8,128)S(1)}, u32[]{:S(2)}, u32[]{:S(2)}) %collective-permute-start.20) | collective-permute-done | bytes 77856 | tf_op jit(solution)/shard_map/ppermute | solution.py:816
  209.9 2.7 %right_factors.1 = (f32[8,192]{1,0:T(8,128)}, f32[8,384]{1,0:T(8,128)}, f32[192,8]{1,0:T(8,128)S(1)}, f32[384,8]{1,0:T(8,128)S(1)}, f32[8,4224]{1,0:T(8,128)S(1)}, /*index=5*/f32[8,1792]{1,0:T(8,128)S(1)}) custom-call(f32[8,2432]{1,0:T(8,128)S(1)} %add.97.refs_0_, f32[8,2432]{1,0:T(8,128)S(1)} %collective-permute-done.20.refs_1_, ...), custom_call_target="tpu_custom_call" | custom-call | flops 5000000000 | bytes 15000000 | tf_op jit(solution)/shard_map/right_factors/pallas_call | solution.py:682
  219.3 4.0 %states_to_vmem.1 = (f32[192,3352]{1,0:T(8,128)S(1)}, f32[192,3352]{1,0:T(8,128)S(1)}, f32[384,768]{1,0:T(8,128)S(1)}, f32[384,768]{1,0:T(8,128)S(1)}) custom-call(f32[192,3352]{1,0:T(8,128)} %refs_0_.1, f32[192,3352]{1,0:T(8,128)} %refs_1_.1, f32[384,768]{1,0:T(8,128)} %refs_2_.2, f32[384,768]{1,0:T(8,128)} %refs_3_.2), custom_call_target="tpu_custom_call" | custom-call | flops 3000000000 | bytes 9000000 | tf_op jit(solution)/shard_map/states_to_vmem/pallas_call | solution.py:768
  223.4 3.4 %collective-permute-start.23 = (f32[8,4224]{1,0:T(8,128)S(1)}, f32[8,4224]{1,0:T(8,128)S(1)}, u32[]{:S(2)}, u32[]{:S(2)}) collective-permute-start(f32[8,4224]{1,0:T(8,128)S(1)} %add.99.refs_0_), channel_id=1, source_target_pairs={{0,4},{1,5},{2,6},{3,7},{4,0},{5,1},{6,2},{7,3},{8,12},{9,13},{10,... | collective-permute-start | bytes 405512 | tf_op jit(solution)/shard_map/ppermute | solution.py:816
  227.5 4.5 %collective-permute-done.23.refs_1_ = f32[8,4224]{1,0:T(8,128)S(1)} collective-permute-done((f32[8,4224]{1,0:T(8,128)S(1)}, f32[8,4224]{1,0:T(8,128)S(1)}, u32[]{:S(2)}, u32[]{:S(2)}) %collective-permute-start.23) | collective-permute-done | bytes 135200 | tf_op jit(solution)/shard_map/ppermute | solution.py:816
  232.0 4.8 %final_update.1 = (f32[8,3352]{1,0:T(8,128)}, f32[192,3352]{1,0:T(8,128)}, f32[192,3352]{1,0:T(8,128)}, f32[192,3352]{1,0:T(8,128)}, f32[8,768]{1,0:T(8,128)}, /...) custom-call(f32[8,4224]{1,0:T(8,128)S(1)} %add.99.refs_0_, ...), custom_call_target="tpu_custom_call" | custom-call | flops 10000000000 | bytes 30000000 | tf_op jit(solution)/shard_map/final_update/pallas_call | solution.py:744
  (115 shorter events, 23.7 us)
Async XLA Ops:
  2.8 20.4 %collective-permute-start.1 = (bf16[192,1816]{1,0:T(8,128)(2,1)S(1)}, bf16[192,1816]{1,0:T(8,128)(2,1)S(1)}, u32[]{:S(2)}, u32[]{:S(2)}) collective-permute-start(bf16[192,1816]{1,0:T(8,128)(2,1)S(1)} %slice.69.refs_9_.refs_14_), channel_id=1, source_target_pairs={{0,16},{8,24},{16,0},{24,8},{1,17},{9,25},{17,1},{25,9},{2,18},{10... | collective-permute-start | bytes 2092040 | tf_op jit(solution)/shard_map/ppermute | solution.py:816
  5.9 41.9 %collective-permute-start = (bf16[192,1816]{1,0:T(8,128)(2,1)S(1)}, bf16[192,1816]{1,0:T(8,128)(2,1)}, u32[]{:S(2)}, u32[]{:S(2)}) collective-permute-start(bf16[192,1816]{1,0:T(8,128)(2,1)S(1)} %slice.69.refs_9_.refs_14_), channel_id=1, source_target_pairs={{0,8},{8,0},{16,24},{24,16},{1,9},{9,1},{17,25},{25,17},{2,10},{10... | collective-permute-start | bytes 2092040 | tf_op jit(solution)/shard_map/ppermute | solution.py:816
  5.9 30.0 %collective-permute-start.4 = (bf16[192,1536]{1,0:T(8,128)(2,1)S(1)}, bf16[192,1536]{1,0:T(8,128)(2,1)}, u32[]{:S(2)}, u32[]{:S(2)}) collective-permute-start(bf16[192,1536]{1,0:T(8,128)(2,1)S(1)} %slice.70.refs_8_.refs_10_), channel_id=1, source_target_pairs={{0,16},{8,24},{16,0},{24,8},{1,17},{9,25},{17,1},{25,9},{2,18},{10... | collective-permute-start | bytes 1769480 | tf_op jit(solution)/shard_map/ppermute | solution.py:816
  6.1 65.9 %collective-permute-start.3 = (bf16[192,1536]{1,0:T(8,128)(2,1)S(1)}, bf16[192,1536]{1,0:T(8,128)(2,1)}, u32[]{:S(2)}, u32[]{:S(2)}) collective-permute-start(bf16[192,1536]{1,0:T(8,128)(2,1)S(1)} %slice.70.refs_8_.refs_10_), channel_id=1, source_target_pairs={{0,8},{8,0},{16,24},{24,16},{1,9},{9,1},{17,25},{25,17},{2,10},{10... | collective-permute-start | bytes 1769480 | tf_op jit(solution)/shard_map/ppermute | solution.py:816
  6.6 41.1 %collective-permute-start.7 = (bf16[384,768]{1,0:T(8,128)(2,1)S(1)}, bf16[384,768]{1,0:T(8,128)(2,1)}, u32[]{:S(2)}, u32[]{:S(2)}) collective-permute-start(bf16[384,768]{1,0:T(8,128)(2,1)S(1)} %convert_element_type.175.refs_12_), channel_id=1, source_target_pairs={{0,16},{8,24},{16,0},{24,8},{1,17},{9,25},{17,1},{25,9},{2,18},{10... | collective-permute-start | bytes 1769480 | tf_op jit(solution)/shard_map/ppermute | solution.py:816
  23.2 25.1 %collective-permute-start.2 = (bf16[192,1816]{1,0:T(8,128)(2,1)S(1)}, bf16[192,1816]{1,0:T(8,128)(2,1)}, u32[]{:S(2)}, u32[]{:S(2)}) collective-permute-start(bf16[192,1816]{1,0:T(8,128)(2,1)S(1)} %collective-permute-done.1.refs_11_.refs_16_), channel_id=1, source_target_pairs={{0,8},{8,0},{16,24},{24,16},{1,9},{9,1},{17,25},{25,17},{2,10},{10... | collective-permute-start | bytes 2092040 | tf_op jit(solution)/shard_map/ppermute | solution.py:816
  35.9 36.0 %collective-permute-start.6 = (bf16[384,768]{1,0:T(8,128)(2,1)S(1)}, bf16[384,768]{1,0:T(8,128)(2,1)S(1)}, u32[]{:S(2)}, u32[]{:S(2)}) collective-permute-start(bf16[384,768]{1,0:T(8,128)(2,1)S(1)} %convert_element_type.175.refs_12_), channel_id=1, source_target_pairs={{0,8},{8,0},{16,24},{24,16},{1,9},{9,1},{17,25},{25,17},{2,10},{10... | collective-permute-start | bytes 1769480 | tf_op jit(solution)/shard_map/ppermute | solution.py:816
  47.7 24.3 %collective-permute-start.5 = (bf16[192,1536]{1,0:T(8,128)(2,1)}, bf16[192,1536]{1,0:T(8,128)(2,1)S(1)}, u32[]{:S(2)}, u32[]{:S(2)}) collective-permute-start(bf16[192,1536]{1,0:T(8,128)(2,1)} %collective-permute-done.4.refs_10_.refs_12_), channel_id=1, source_target_pairs={{0,8},{8,0},{16,24},{24,16},{1,9},{9,1},{17,25},{25,17},{2,10},{10... | collective-permute-start | bytes 1769480 | tf_op jit(solution)/shard_map/ppermute | solution.py:816
  47.7 24.3 %collective-permute-start.8 = (bf16[384,768]{1,0:T(8,128)(2,1)}, bf16[384,768]{1,0:T(8,128)(2,1)S(1)}, u32[]{:S(2)}, u32[]{:S(2)}) collective-permute-start(bf16[384,768]{1,0:T(8,128)(2,1)} %collective-permute-done.7.refs_14_), channel_id=1, source_target_pairs={{0,8},{8,0},{16,24},{24,16},{1,9},{9,1},{17,25},{25,17},{2,10},{10... | collective-permute-start | bytes 1769480 | tf_op jit(solution)/shard_map/ppermute | solution.py:816
  94.3 50.9 %collective-permute-start.15 = (bf16[384,768]{1,0:T(8,128)(2,1)S(1)}, bf16[384,768]{1,0:T(8,128)(2,1)S(1)}, u32[]{:S(2)}, u32[]{:S(2)}) collective-permute-start(bf16[384,768]{1,0:T(8,128)(2,1)S(1)} %get-tuple-element.139), channel_id=1, source_target_pairs={{0,8},{8,0},{16,24},{24,16},{1,9},{9,1},{17,25},{25,17},{2,10},{10... | collective-permute-start | bytes 1769480 | tf_op jit(solution)/shard_map/ppermute | solution.py:816
  94.4 51.1 %collective-permute-start.16 = (bf16[384,768]{1,0:T(8,128)(2,1)S(1)}, bf16[384,768]{1,0:T(8,128)(2,1)S(1)}, u32[]{:S(2)}, u32[]{:S(2)}) collective-permute-start(bf16[384,768]{1,0:T(8,128)(2,1)S(1)} %get-tuple-element.138), channel_id=1, source_target_pairs={{0,8},{8,0},{16,24},{24,16},{1,9},{9,1},{17,25},{25,17},{2,10},{10... | collective-permute-start | bytes 1769480 | tf_op jit(solution)/shard_map/ppermute | solution.py:816
  98.6 49.0 %collective-permute-start.10 = (bf16[192,1536]{1,0:T(8,128)(2,1)S(1)}, bf16[192,1536]{1,0:T(8,128)(2,1)S(1)}, u32[]{:S(2)}, u32[]{:S(2)}) collective-permute-start(bf16[192,1536]{1,0:T(8,128)(2,1)S(1)} %get-tuple-element.142), channel_id=1, source_target_pairs={{0,8},{8,0},{16,24},{24,16},{1,9},{9,1},{17,25},{25,17},{2,10},{10... | collective-permute-start | bytes 1769480 | tf_op jit(solution)/shard_map/ppermute | solution.py:816
  98.7 48.9 %collective-permute-start.9 = (bf16[192,1536]{1,0:T(8,128)(2,1)S(1)}, bf16[192,1536]{1,0:T(8,128)(2,1)S(1)}, u32[]{:S(2)}, u32[]{:S(2)}) collective-permute-start(bf16[192,1536]{1,0:T(8,128)(2,1)S(1)} %get-tuple-element.143), channel_id=1, source_target_pairs={{0,8},{8,0},{16,24},{24,16},{1,9},{9,1},{17,25},{25,17},{2,10},{10... | collective-permute-start | bytes 1769480 | tf_op jit(solution)/shard_map/ppermute | solution.py:816
  144.9 3.4 %collective-permute-start.12 = (bf16[192,1816]{1,0:T(8,128)(2,1)S(1)}, bf16[192,1816]{1,0:T(8,128)(2,1)S(1)}, u32[]{:S(2)}, u32[]{:S(2)}) collective-permute-start(bf16[192,1816]{1,0:T(8,128)(2,1)S(1)} %get-tuple-element.135), channel_id=1, source_target_pairs={{0,8},{8,0},{16,24},{24,16},{1,9},{9,1},{17,25},{25,17},{2,10},{10... | collective-permute-start | bytes 2092040 | tf_op jit(solution)/shard_map/ppermute | solution.py:816
  145.8 19.3 %collective-permute-start.17 = (bf16[384,768]{1,0:T(8,128)(2,1)S(1)}, bf16[384,768]{1,0:T(8,128)(2,1)S(1)}, u32[]{:S(2)}, u32[]{:S(2)}) collective-permute-start(bf16[384,768]{1,0:T(8,128)(2,1)S(1)} %get-tuple-element.136), channel_id=1, source_target_pairs={{0,16},{8,24},{16,0},{24,8},{1,17},{9,25},{17,1},{25,9},{2,18},{10... | collective-permute-start | bytes 1769480 | tf_op jit(solution)/shard_map/ppermute | solution.py:816
  147.9 26.8 %collective-permute-start.11 = (bf16[192,1536]{1,0:T(8,128)(2,1)S(1)}, bf16[192,1536]{1,0:T(8,128)(2,1)S(1)}, u32[]{:S(2)}, u32[]{:S(2)}) collective-permute-start(bf16[192,1536]{1,0:T(8,128)(2,1)S(1)} %get-tuple-element.140), channel_id=1, source_target_pairs={{0,16},{8,24},{16,0},{24,8},{1,17},{9,25},{17,1},{25,9},{2,18},{10... | collective-permute-start | bytes 1769480 | tf_op jit(solution)/shard_map/ppermute | solution.py:816
  148.7 41.1 %collective-permute-start.14 = (bf16[192,1816]{1,0:T(8,128)(2,1)S(1)}, bf16[192,1816]{1,0:T(8,128)(2,1)S(1)}, u32[]{:S(2)}, u32[]{:S(2)}) collective-permute-start(bf16[192,1816]{1,0:T(8,128)(2,1)S(1)} %get-tuple-element.132), channel_id=1, source_target_pairs={{0,16},{8,24},{16,0},{24,8},{1,17},{9,25},{17,1},{25,9},{2,18},{10... | collective-permute-start | bytes 2092040 | tf_op jit(solution)/shard_map/ppermute | solution.py:816
  195.3 4.4 %collective-permute-start.18 = (f32[8,2432]{1,0:T(8,128)S(1)}, f32[8,2432]{1,0:T(8,128)S(1)}, u32[]{:S(2)}, u32[]{:S(2)}) collective-permute-start(f32[8,2432]{1,0:T(8,128)S(1)} %get-tuple-element.99), channel_id=1, source_target_pairs={{0,1},{1,0},{2,3},{3,2},{4,5},{5,4},{6,7},{7,6},{8,9},{9,8},{10,11... | collective-permute-start | bytes 233480 | tf_op jit(solution)/shard_map/ppermute | solution.py:816
  199.7 4.5 %collective-permute-start.19 = (f32[8,2432]{1,0:T(8,128)S(1)}, f32[8,2432]{1,0:T(8,128)S(1)}, u32[]{:S(2)}, u32[]{:S(2)}) collective-permute-start(f32[8,2432]{1,0:T(8,128)S(1)} %add.96), channel_id=1, source_target_pairs={{0,2},{1,3},{2,0},{3,1},{4,6},{5,7},{6,4},{7,5},{8,10},{9,11},{10,... | collective-permute-start | bytes 233480 | tf_op jit(solution)/shard_map/ppermute | solution.py:816
  204.2 5.7 %collective-permute-start.20 = (f32[8,2432]{1,0:T(8,128)S(1)}, f32[8,2432]{1,0:T(8,128)S(1)}, u32[]{:S(2)}, u32[]{:S(2)}) collective-permute-start(f32[8,2432]{1,0:T(8,128)S(1)} %add.97.refs_0_), channel_id=1, source_target_pairs={{0,4},{1,5},{2,6},{3,7},{4,0},{5,1},{6,2},{7,3},{8,12},{9,13},{10,... | collective-permute-start | bytes 233480 | tf_op jit(solution)/shard_map/ppermute | solution.py:816
  212.6 5.0 %collective-permute-start.21 = (f32[8,4224]{1,0:T(8,128)S(1)}, f32[8,4224]{1,0:T(8,128)S(1)}, u32[]{:S(2)}, u32[]{:S(2)}) collective-permute-start(f32[8,4224]{1,0:T(8,128)S(1)} %get-tuple-element.104), channel_id=1, source_target_pairs={{0,1},{1,0},{2,3},{3,2},{4,5},{5,4},{6,7},{7,6},{8,9},{9,8},{10,11... | collective-permute-start | bytes 405512 | tf_op jit(solution)/shard_map/ppermute | solution.py:816
  215.3 11.4 %collective-permute-start.25 = (f32[8,1792]{1,0:T(8,128)S(1)}, f32[8,1792]{1,0:T(8,128)S(1)}, u32[]{:S(2)}, u32[]{:S(2)}) collective-permute-start(f32[8,1792]{1,0:T(8,128)S(1)} %add.100.refs_0_), channel_id=1, source_target_pairs={{0,16},{8,24},{16,0},{24,8},{1,17},{9,25},{17,1},{25,9},{2,18},{10... | collective-permute-start | bytes 172040 | tf_op jit(solution)/shard_map/ppermute | solution.py:816
  217.7 5.7 %collective-permute-start.22 = (f32[8,4224]{1,0:T(8,128)S(1)}, f32[8,4224]{1,0:T(8,128)S(1)}, u32[]{:S(2)}, u32[]{:S(2)}) collective-permute-start(f32[8,4224]{1,0:T(8,128)S(1)} %add.98), channel_id=1, source_target_pairs={{0,2},{1,3},{2,0},{3,1},{4,6},{5,7},{6,4},{7,5},{8,10},{9,11},{10,... | collective-permute-start | bytes 405512 | tf_op jit(solution)/shard_map/ppermute | solution.py:816
  223.4 8.7 %collective-permute-start.23 = (f32[8,4224]{1,0:T(8,128)S(1)}, f32[8,4224]{1,0:T(8,128)S(1)}, u32[]{:S(2)}, u32[]{:S(2)}) collective-permute-start(f32[8,4224]{1,0:T(8,128)S(1)} %add.99.refs_0_), channel_id=1, source_target_pairs={{0,4},{1,5},{2,6},{3,7},{4,0},{5,1},{6,2},{7,3},{8,12},{9,13},{10,... | collective-permute-start | bytes 405512 | tf_op jit(solution)/shard_map/ppermute | solution.py:816
  (17 other events, 217.1 us)
